TPU v7x, 32 devices: a whole 2x2x4 slice. The times are simulated.
32 devices in a mesh: dp: 4 (over y, x), seq: 8 (over z, core).
Axes of the slice: x: 2, y: 2, z: 4, core: 2. Of those that a mesh axis runs over, the one named last changes fastest.
Arguments:
- inputs: bfloat16 [8, 1536, 768], P('dp', 'seq'), may hold values from -6 to 6
- segments: int32 [8, 1536], P('dp'), may hold values from 0 to 5, never falling along the last dimension, each value on 1 to 1152 neighbouring positions
- rand_blocks: int32 [8, 24, 12, 3], P('dp'), may hold values from 0 to 23, as said below
- w_qkv: bfloat16 [768, 2304], P('dp'), may hold values from -0.21875 to 0.21875
- w_out: bfloat16 [768, 768], P('dp'), may hold values from -1.75 to 1.75
- w_up: bfloat16 [768, 3072], P('dp'), may hold values from -0.21875 to 0.21875
- w_down: bfloat16 [3072, 768], P('dp'), may hold values from -0.109375 to 0.109375
- norm_gain: float32 [2, 768], replicated, may hold values from 0.5 to 1.5
- norm_bias: float32 [2, 768], replicated, may hold values from -3 to 3
- out_grad: bfloat16 [8, 1536, 768], P('dp', 'seq'), may hold values from -6 to 6
Outputs:
- output: bfloat16 [8, 1536, 768], P('dp', 'seq')
- input_grad: float32 [8, 1536, 768], P('dp', 'seq')
- w_qkv_grad: float32 [768, 2304], P(('dp', 'seq'))
- w_out_grad: float32 [768, 768], P(('dp', 'seq'))
- w_up_grad: float32 [768, 3072], P(('dp', 'seq'))
- w_down_grad: float32 [3072, 768], P(('dp', 'seq'))
- norm_gain_grad: float32 [2, 768], P(None, ('dp', 'seq'))
- norm_bias_grad: float32 [2, 768], P(None, ('dp', 'seq'))
Inputs may be any that keep to these rules, and one draw needn't show every extreme that they name: `rand_blocks`: for every sequence and every index t of seq, among the 108 entries of the query blocks t * 3 .. (t + 1) * 3 - 1, at most 14 name key blocks held by one index of seq (key block // 3), and some index is named exactly 14 times.
All inputs are finite; a program needn't handle non-finite values.
Results may differ from a plain program's by a relative error of at most 0.013.
Values may be sent and summed in bfloat16 or wider, within the bound.
A program may use at most 192 MiB of HBM per device.

v0:
```python
import functools
import jax
import jax.numpy as jnp
import numpy as np
from jax import lax
from jax.experimental import pallas as pl
from jax.experimental.pallas import tpu as pltpu
from jax.sharding import PartitionSpec as P

H = 12
HEAD = 64
BLOCK = 64
R = 3
MICRO = 2


norm_eps = 1e-05
masked_score = -1e30
root_half = 0.7071067811865476
inv_root_two_pi = 0.3989422804014327


def padded(cells, sides, width):
    for axis, dim in sides:
        count = lax.axis_size(axis)
        ends = count - 1
        head = lax.slice_in_dim(cells, 0, width, axis=dim)
        tail = lax.slice_in_dim(cells, cells.shape[dim] - width, cells.shape[dim], axis=dim)
        cells = jnp.concatenate(
            [
                lax.ppermute(tail, axis, [(i, (i + 1) % count) for i in range(ends)]),
                cells,
                lax.ppermute(head, axis, [((i + 1) % count, i) for i in range(ends)]),
            ],
            axis=dim,
        )
    return cells


def from_root(x, axis, root):
    mine = lax.axis_index(axis) == root
    return lax.psum(jnp.where(mine, x, jnp.zeros_like(x)), axis)


def merged(x, axis, combine):
    everything = jax.tree.map(lambda part: lax.all_gather(part, axis), x)
    initial = jax.tree.map(lambda part: part[0], everything)

    def step(k, so_far):
        return combine(so_far, jax.tree.map(lambda part: part[k], everything))

    return lax.fori_loop(1, lax.axis_size(axis), step, initial)


def product(left_side, right_side):
    return jnp.dot(left_side, right_side, preferred_element_type=jnp.float32)


def product_tn(left_side, right_side):
    return lax.dot_general(
        left_side, right_side, (((0,), (0,)), ((), ())), preferred_element_type=jnp.float32
    )


def product_nt(left_side, right_side):
    return lax.dot_general(
        left_side, right_side, (((1,), (1,)), ((), ())), preferred_element_type=jnp.float32
    )


def gelu_value(pre_act):
    return 0.5 * pre_act * (1.0 + lax.erf(pre_act * root_half))


def gelu_slope(pre_act):
    return (
        0.5 * (1.0 + lax.erf(pre_act * root_half))
        + pre_act * jnp.exp(-0.5 * pre_act * pre_act) * inv_root_two_pi
    )


def norm_forward(residual, gain_row, shift_row):
    mean_row = jnp.mean(residual, axis=-1, keepdims=True)
    centred = residual - mean_row
    variance = jnp.mean(centred * centred, axis=-1, keepdims=True)
    inv_std = lax.rsqrt(variance + norm_eps)
    normed = centred * inv_std
    return (normed * gain_row + shift_row, normed, inv_std)


def norm_backward(grad_rows, normed, inv_std, gain_row):
    scaled = grad_rows * gain_row
    back_rows = inv_std * (
        scaled
        - jnp.mean(scaled, axis=-1, keepdims=True)
        - normed * jnp.mean(scaled * normed, axis=-1, keepdims=True)
    )
    return (back_rows, jnp.sum(grad_rows * normed, axis=0), jnp.sum(grad_rows, axis=0))


def merge_stats(first_pair, second_pair):
    joint_max = jnp.maximum(first_pair[0], second_pair[0])
    joint_sum = first_pair[1] * jnp.exp(first_pair[0] - joint_max) + second_pair[1] * jnp.exp(
        second_pair[0] - joint_max
    )
    return (joint_max, joint_sum)


def local_scores(query_heads, shared_keys, random_keys, shared_ok, random_ok, scale_factor):
    part_shared = jnp.einsum(
        "sbqhd,sbkhd->sbhqk", query_heads, shared_keys, preferred_element_type=jnp.float32
    )
    part_random = jnp.einsum(
        "sbqhd,sbhkd->sbhqk", query_heads, random_keys, preferred_element_type=jnp.float32
    )
    scores = jnp.concatenate([part_shared, part_random], axis=4) * scale_factor
    allowed = jnp.concatenate(
        [jnp.broadcast_to(shared_ok[:, :, None], part_shared.shape), random_ok], axis=4
    )
    return jnp.where(allowed, scores, masked_score)


def per_device(
    inputs, segments, rand_blocks, w_qkv, w_out, w_up, w_down, norm_gain, norm_bias, out_grad
):
    seq_total, tok_dev, features = inputs.shape
    devices = lax.axis_size("seq")
    my_index = lax.axis_index("seq")
    blocks_dev = tok_dev // BLOCK
    blocks_all = blocks_dev * devices
    entries = blocks_dev * H * R
    capacity = max(2, entries // devices + 1)
    per_micro = seq_total // MICRO
    glob_rows = 2 * BLOCK
    shared_count = 5 * BLOCK
    scale_factor = HEAD ** (-0.5)
    token_rows = per_micro * tok_dev
    owner_flag = (my_index == 0).astype(jnp.float32)
    row_global = my_index * tok_dev + jnp.arange(tok_dev, dtype=jnp.int32) < glob_rows
    window_index = np.arange(blocks_dev)[:, None] + np.arange(3)[None, :]
    win_blocks = (
        my_index * blocks_dev
        + jnp.arange(blocks_dev, dtype=jnp.int32)[:, None]
        + jnp.arange(-1, 2, dtype=jnp.int32)[None, :]
    )
    win_inside = (win_blocks >= 0) & (win_blocks < blocks_all)
    win_clipped = jnp.clip(win_blocks, 0, blocks_all - 1)
    entry_heads = jnp.arange(entries, dtype=jnp.int32) // R % H
    slot_ids = jnp.arange(capacity, dtype=jnp.int32)
    earlier = jnp.arange(entries)[None, :] < jnp.arange(entries)[:, None]
    seq_ids = jnp.arange(per_micro, dtype=jnp.int32)
    grad_qkv_w = jnp.zeros((features, 3 * features), jnp.float32)
    grad_out_w = jnp.zeros((features, features), jnp.float32)
    grad_up_w = jnp.zeros((features, w_up.shape[1]), jnp.float32)
    grad_down_w = jnp.zeros((w_down.shape[0] * lax.axis_size("dp"), features), jnp.float32)
    gain_acc = jnp.zeros((2, features), jnp.float32)
    shift_acc = jnp.zeros((2, features), jnp.float32)
    output_parts = []
    input_parts = []
    for micro_step in range(MICRO):
        start_seq = micro_step * per_micro
        tokens_in = inputs[start_seq : start_seq + per_micro]
        seg_micro = segments[start_seq : start_seq + per_micro]
        rand_micro = rand_blocks[start_seq : start_seq + per_micro]
        cotangent = out_grad[start_seq : start_seq + per_micro]
        full_qkv, full_out, full_up, full_down = (
            lax.all_gather(w_qkv, "dp", axis=0, tiled=True),
            lax.all_gather(w_out, "dp", axis=0, tiled=True),
            lax.all_gather(w_up, "dp", axis=0, tiled=True),
            lax.all_gather(w_down, "dp", axis=0, tiled=True),
        )
        tokens_flat = tokens_in.reshape(token_rows, features)
        qkv_rows = (
            product(tokens_flat, full_qkv)
            .astype(jnp.bfloat16)
            .reshape(per_micro, tok_dev, 3 * features)
        )
        queries = qkv_rows[..., :features]
        keyvals = qkv_rows[..., features:]
        extended = padded(keyvals, (("seq", 1),), BLOCK)
        global_block = from_root(qkv_rows[:, :glob_rows], "seq", 0)
        requests = rand_micro.reshape(per_micro, devices, entries)
        owners = requests // blocks_dev
        local_block = requests % blocks_dev
        same_owner = owners[:, :, :, None] == owners[:, :, None, :]
        slot_rank = jnp.sum(same_owner & earlier[None, None], axis=3)
        slot_hit = ((owners == my_index)[..., None] & (slot_rank[..., None] == slot_ids)).astype(
            jnp.int32
        )
        slot_live = jnp.sum(slot_hit, axis=2)
        slot_piece = jnp.sum(slot_hit * (local_block * H + entry_heads)[..., None], axis=2)
        piece_index = jnp.transpose(slot_piece, (1, 2, 0))
        live_mask = jnp.transpose(slot_live, (1, 2, 0))
        pieces = (
            keyvals.reshape(per_micro, blocks_dev, BLOCK, 2, H, HEAD)
            .transpose(0, 1, 4, 2, 3, 5)
            .reshape(per_micro, blocks_dev * H, BLOCK, 2 * HEAD)
        )
        outgoing = pieces[seq_ids[None, None, :], piece_index]
        outgoing = jnp.where(live_mask[..., None, None] > 0, outgoing, jnp.zeros((), jnp.bfloat16))
        outgoing = outgoing.reshape(devices * capacity, per_micro, BLOCK, 2 * HEAD)
        incoming = lax.all_to_all(outgoing, "seq", split_axis=0, concat_axis=0, tiled=True)
        my_owner = jnp.take(owners, my_index, axis=1)
        my_rank = jnp.take(slot_rank, my_index, axis=1)
        my_request = jnp.take(requests, my_index, axis=1)
        positions = my_owner * capacity + my_rank
        fetched = incoming[positions, seq_ids[:, None]].reshape(
            per_micro, blocks_dev, H, R, BLOCK, 2, HEAD
        )
        random_keys = fetched[..., 0, :].reshape(per_micro, blocks_dev, H, R * BLOCK, HEAD)
        random_vals = fetched[..., 1, :].reshape(per_micro, blocks_dev, H, R * BLOCK, HEAD)
        seg_blocks = seg_micro.reshape(per_micro, blocks_all, BLOCK)
        query_seg = lax.dynamic_slice_in_dim(seg_micro, my_index * tok_dev, tok_dev, 1).reshape(
            per_micro, blocks_dev, BLOCK
        )
        window_seg = seg_blocks[:, win_clipped].reshape(per_micro, blocks_dev, 3 * BLOCK)
        window_ok = (query_seg[..., :, None] == window_seg[:, :, None, :]) & jnp.repeat(
            win_inside, BLOCK, axis=1
        )[None, :, None, :]
        shared_ok = jnp.concatenate(
            [window_ok, jnp.ones((per_micro, blocks_dev, BLOCK, glob_rows), bool)], axis=3
        )
        random_seg = seg_blocks[seq_ids[:, None], my_request].reshape(
            per_micro, blocks_dev, H, R * BLOCK
        )
        random_ok = query_seg[:, :, None, :, None] == random_seg[:, :, :, None, :]
        ext_blocks = extended.reshape(per_micro, blocks_dev + 2, BLOCK, 2 * features)
        window_kv = ext_blocks[:, window_index].reshape(
            per_micro, blocks_dev, 3 * BLOCK, 2 * features
        )
        glob_kv = jnp.broadcast_to(
            global_block[:, None, :, features:], (per_micro, blocks_dev, glob_rows, 2 * features)
        )
        shared_kv = jnp.concatenate([window_kv, glob_kv], axis=2)
        shared_keys = shared_kv[..., :features].reshape(
            per_micro, blocks_dev, shared_count, H, HEAD
        )
        shared_vals = shared_kv[..., features:].reshape(
            per_micro, blocks_dev, shared_count, H, HEAD
        )
        query_heads = queries.reshape(per_micro, blocks_dev, BLOCK, H, HEAD)
        scores = local_scores(
            query_heads, shared_keys, random_keys, shared_ok, random_ok, scale_factor
        )
        row_max = jnp.max(scores, axis=4, keepdims=True)
        exp_terms = jnp.exp(scores - row_max)
        row_sum = jnp.sum(exp_terms, axis=4, keepdims=True)
        local_probs = exp_terms / row_sum
        log_norm = row_max + jnp.log(row_sum)
        local_weights = local_probs.astype(jnp.bfloat16)
        local_att = jnp.einsum(
            "sbhqk,sbkhd->sbqhd",
            local_weights[..., :shared_count],
            shared_vals,
            preferred_element_type=jnp.float32,
        )
        local_att = local_att + jnp.einsum(
            "sbhqk,sbhkd->sbqhd",
            local_weights[..., shared_count:],
            random_vals,
            preferred_element_type=jnp.float32,
        )
        local_att = local_att.reshape(per_micro, tok_dev, features)
        glob_query = global_block[..., :features].reshape(per_micro, glob_rows, H, HEAD)
        local_keys = keyvals[..., :features].reshape(per_micro, tok_dev, H, HEAD)
        local_vals = keyvals[..., features:].reshape(per_micro, tok_dev, H, HEAD)
        glob_scores = (
            jnp.einsum(
                "sqhd,skhd->shqk", glob_query, local_keys, preferred_element_type=jnp.float32
            )
            * scale_factor
        )
        part_max = jnp.max(glob_scores, axis=3)
        part_sum = jnp.sum(jnp.exp(glob_scores - part_max[..., None]), axis=3)
        glob_max, glob_sum = merged((part_max, part_sum), "seq", merge_stats)
        glob_lse = glob_max + jnp.log(glob_sum)
        glob_probs = jnp.exp(glob_scores - glob_lse[..., None])
        glob_weights = glob_probs.astype(jnp.bfloat16)
        glob_part = jnp.einsum(
            "shqk,skhd->sqhd", glob_weights, local_vals, preferred_element_type=jnp.float32
        ).reshape(per_micro, glob_rows, features)
        glob_out = lax.psum(glob_part, "seq")
        glob_full = jnp.concatenate(
            [glob_out, jnp.zeros((per_micro, tok_dev - glob_rows, features), jnp.float32)], axis=1
        )
        attention = jnp.where(row_global[None, :, None], glob_full, local_att).astype(jnp.bfloat16)
        att_flat = attention.reshape(token_rows, features)
        resid_one = tokens_flat.astype(jnp.float32) + product(att_flat, full_out)
        hidden_one, normed_one, inv_one = norm_forward(resid_one, norm_gain[0], norm_bias[0])
        hidden_low = hidden_one.astype(jnp.bfloat16)
        pre_act = product(hidden_low, full_up)
        activated = gelu_value(pre_act).astype(jnp.bfloat16)
        resid_two = hidden_one + product(activated, full_down)
        result, normed_two, inv_two = norm_forward(resid_two, norm_gain[1], norm_bias[1])
        output_parts.append(result.astype(jnp.bfloat16).reshape(per_micro, tok_dev, features))
        grad_rows = cotangent.reshape(token_rows, features).astype(jnp.float32)
        grad_resid_two, gain_two, shift_two = norm_backward(
            grad_rows, normed_two, inv_two, norm_gain[1]
        )
        grad_branch = grad_resid_two.astype(jnp.bfloat16)
        grad_down_w = grad_down_w + product_tn(activated, grad_branch)
        grad_pre = (product_nt(grad_branch, full_down) * gelu_slope(pre_act)).astype(jnp.bfloat16)
        grad_up_w = grad_up_w + product_tn(hidden_low, grad_pre)
        grad_hidden = grad_resid_two + product_nt(grad_pre, full_up)
        grad_resid_one, gain_one, shift_one = norm_backward(
            grad_hidden, normed_one, inv_one, norm_gain[0]
        )
        grad_mix = grad_resid_one.astype(jnp.bfloat16)
        grad_out_w = grad_out_w + product_tn(att_flat, grad_mix)
        grad_att = (
            product_nt(grad_mix, full_out)
            .astype(jnp.bfloat16)
            .reshape(per_micro, tok_dev, features)
        )
        gain_acc = gain_acc + jnp.stack([gain_one, gain_two])
        shift_acc = shift_acc + jnp.stack([shift_one, shift_two])
        grad_local = jnp.where(
            row_global[None, :, None], jnp.zeros((), jnp.bfloat16), grad_att
        ).reshape(per_micro, blocks_dev, BLOCK, H, HEAD)
        scores = local_scores(
            query_heads, shared_keys, random_keys, shared_ok, random_ok, scale_factor
        )
        local_probs = jnp.exp(scores - log_norm)
        local_weights = local_probs.astype(jnp.bfloat16)
        grad_prob = jnp.concatenate(
            [
                jnp.einsum(
                    "sbqhd,sbkhd->sbhqk",
                    grad_local,
                    shared_vals,
                    preferred_element_type=jnp.float32,
                ),
                jnp.einsum(
                    "sbqhd,sbhkd->sbhqk",
                    grad_local,
                    random_vals,
                    preferred_element_type=jnp.float32,
                ),
            ],
            axis=4,
        )
        row_delta = jnp.sum(local_probs * grad_prob, axis=4, keepdims=True)
        grad_score = (local_probs * (grad_prob - row_delta)).astype(jnp.bfloat16)
        grad_query = jnp.einsum(
            "sbhqk,sbkhd->sbqhd",
            grad_score[..., :shared_count],
            shared_keys,
            preferred_element_type=jnp.float32,
        )
        grad_query = (
            grad_query
            + jnp.einsum(
                "sbhqk,sbhkd->sbqhd",
                grad_score[..., shared_count:],
                random_keys,
                preferred_element_type=jnp.float32,
            )
        ) * scale_factor
        grad_key_shared = (
            jnp.einsum(
                "sbhqk,sbqhd->sbkhd",
                grad_score[..., :shared_count],
                query_heads,
                preferred_element_type=jnp.float32,
            )
            * scale_factor
        )
        grad_val_shared = jnp.einsum(
            "sbhqk,sbqhd->sbkhd",
            local_weights[..., :shared_count],
            grad_local,
            preferred_element_type=jnp.float32,
        )
        grad_key_random = (
            jnp.einsum(
                "sbhqk,sbqhd->sbhkd",
                grad_score[..., shared_count:],
                query_heads,
                preferred_element_type=jnp.float32,
            )
            * scale_factor
        )
        grad_val_random = jnp.einsum(
            "sbhqk,sbqhd->sbhkd",
            local_weights[..., shared_count:],
            grad_local,
            preferred_element_type=jnp.float32,
        )
        grad_shared = jnp.concatenate(
            [
                grad_key_shared.reshape(per_micro, blocks_dev, shared_count, features),
                grad_val_shared.reshape(per_micro, blocks_dev, shared_count, features),
            ],
            axis=3,
        )
        grad_window = grad_shared[:, :, : 3 * BLOCK].reshape(
            per_micro, blocks_dev, 3, BLOCK, 2 * features
        )
        ext_grad = jnp.zeros((per_micro, blocks_dev + 2, BLOCK, 2 * features), jnp.float32)
        for offset in range(3):
            ext_grad = ext_grad.at[:, offset : offset + blocks_dev].add(grad_window[:, :, offset])
        grad_glob_keys = jnp.sum(grad_shared[:, :, 3 * BLOCK :], axis=1)
        grad_random = jnp.stack([grad_key_random, grad_val_random], axis=4).reshape(
            per_micro, entries, BLOCK, 2 * HEAD
        )
        returned = (
            jnp.zeros((devices * capacity, per_micro, BLOCK, 2 * HEAD), jnp.float32)
            .at[positions, seq_ids[:, None]]
            .set(grad_random)
        )
        arrived = lax.all_to_all(
            returned.astype(jnp.bfloat16), "seq", split_axis=0, concat_axis=0, tiled=True
        ).astype(returned.dtype)
        arrived = arrived.reshape(devices, capacity, per_micro, BLOCK, 2 * HEAD) * live_mask[
            ..., None, None
        ].astype(jnp.float32)
        piece_grad = (
            jnp.zeros((per_micro, blocks_dev * H, BLOCK, 2 * HEAD), jnp.float32)
            .at[seq_ids[None, None, :], piece_index]
            .add(arrived)
        )
        piece_grad = (
            piece_grad.reshape(per_micro, blocks_dev, H, BLOCK, 2, HEAD)
            .transpose(0, 1, 3, 4, 2, 5)
            .reshape(per_micro, tok_dev, 2 * features)
        )
        rim_pair = jnp.concatenate([ext_grad[:, 0], ext_grad[:, blocks_dev + 1]], axis=1)
        rim_back = padded(rim_pair.astype(jnp.bfloat16), (("seq", 1),), BLOCK).astype(
            rim_pair.dtype
        )
        grad_kv = (
            ext_grad[:, 1 : blocks_dev + 1].reshape(per_micro, tok_dev, 2 * features) + piece_grad
        )
        grad_kv = grad_kv.at[:, :BLOCK].add(rim_back[:, :BLOCK])
        grad_kv = grad_kv.at[:, tok_dev - BLOCK :].add(rim_back[:, 3 * BLOCK :])
        grad_glob = from_root(grad_att[:, :glob_rows], "seq", 0)
        grad_glob_heads = grad_glob.reshape(per_micro, glob_rows, H, HEAD)
        glob_scores = (
            jnp.einsum(
                "sqhd,skhd->shqk", glob_query, local_keys, preferred_element_type=jnp.float32
            )
            * scale_factor
        )
        glob_probs = jnp.exp(glob_scores - glob_lse[..., None])
        glob_weights = glob_probs.astype(jnp.bfloat16)
        glob_grad_prob = jnp.einsum(
            "sqhd,skhd->shqk", grad_glob_heads, local_vals, preferred_element_type=jnp.float32
        )
        glob_delta = lax.psum(jnp.sum(glob_probs * glob_grad_prob, axis=3), "seq")
        glob_grad_score = (glob_probs * (glob_grad_prob - glob_delta[..., None])).astype(
            jnp.bfloat16
        )
        glob_grad_query = (
            jnp.einsum(
                "shqk,skhd->sqhd", glob_grad_score, local_keys, preferred_element_type=jnp.float32
            )
            * scale_factor
        )
        glob_grad_key = (
            jnp.einsum(
                "shqk,sqhd->skhd", glob_grad_score, glob_query, preferred_element_type=jnp.float32
            )
            * scale_factor
        )
        glob_grad_val = jnp.einsum(
            "shqk,sqhd->skhd", glob_weights, grad_glob_heads, preferred_element_type=jnp.float32
        )
        grad_kv = grad_kv + jnp.concatenate(
            [
                glob_grad_key.reshape(per_micro, tok_dev, features),
                glob_grad_val.reshape(per_micro, tok_dev, features),
            ],
            axis=2,
        )
        summed_query, summed_keys = lax.psum(
            (glob_grad_query.reshape(per_micro, glob_rows, features), grad_glob_keys), "seq"
        )
        grad_kv = grad_kv.at[:, :glob_rows].add(owner_flag * summed_keys)
        grad_queries = (
            grad_query.reshape(per_micro, tok_dev, features)
            .at[:, :glob_rows]
            .add(owner_flag * summed_query)
        )
        grad_qkv_rows = (
            jnp.concatenate([grad_queries, grad_kv], axis=2)
            .astype(jnp.bfloat16)
            .reshape(token_rows, 3 * features)
        )
        grad_qkv_w = grad_qkv_w + product_tn(tokens_flat, grad_qkv_rows)
        input_rows = grad_resid_one + product_nt(grad_qkv_rows, full_qkv)
        input_parts.append(input_rows.reshape(per_micro, tok_dev, features))
    summed = (
        lax.psum_scatter(grad_qkv_w, ("dp", "seq"), scatter_dimension=0, tiled=True),
        lax.psum_scatter(grad_out_w, ("dp", "seq"), scatter_dimension=0, tiled=True),
        lax.psum_scatter(grad_up_w, ("dp", "seq"), scatter_dimension=0, tiled=True),
        lax.psum_scatter(grad_down_w, ("dp", "seq"), scatter_dimension=0, tiled=True),
        lax.psum_scatter(gain_acc, ("dp", "seq"), scatter_dimension=1, tiled=True),
        lax.psum_scatter(shift_acc, ("dp", "seq"), scatter_dimension=1, tiled=True),
    )
    return (
        jnp.concatenate(output_parts, axis=0),
        jnp.concatenate(input_parts, axis=0),
        summed[0],
        summed[1],
        summed[2],
        summed[3],
        summed[4],
        summed[5],
    )


TILE = 128
NH = 3
CH = 256
LOG2E = 1.4426950408889634
SCALE2 = HEAD ** (-0.5) * LOG2E
NEG = -1e30
F32 = jnp.float32
BF16 = jnp.bfloat16


def nt(a, b):
    return lax.dot_general(a, b, (((1,), (1,)), ((), ())), preferred_element_type=F32)


def nn(a, b):
    return jnp.dot(a, b, preferred_element_type=F32)


MESH = pl.DeviceIdType.MESH
ANYSPACE = pl.BlockSpec(memory_space=pl.ANY)
VMEMSPACE = pl.BlockSpec(memory_space=pltpu.VMEM)


class Copies:
    def __init__(self, send, recv):
        self.send = send
        self.recv = recv
        self.used = 0

    def to(self, src, dst, device):
        index = self.used
        self.used += 1
        return pltpu.make_async_remote_copy(
            src_ref=src, dst_ref=dst, send_sem=self.send.at[index], recv_sem=self.recv.at[index],
            device_id=device, device_id_type=MESH,
        )


class Place:
    def __init__(self):
        self.d = lax.axis_index("dp")
        self.t = lax.axis_index("seq")
        self.x = lax.rem(self.d, 2)
        self.y = self.d // 2
        self.c = lax.rem(self.t, 2)
        self.z = self.t // 2
        self.half = self.z // 2
        self.xn = self.d + 1 - 2 * self.x
        self.yn = self.d + 2 - 4 * self.y
        self.diag = 3 - self.d
        self.pair_z = self.z + 1 - 2 * lax.rem(self.z, 2)
        self.across_x = (self.xn, self.t)
        self.across_y = (self.yn, self.t)
        self.partner = (self.d, self.t + 1 - 2 * self.c)

    def at_z(self, z):
        return (self.d, 2 * z + self.c)


def meet(devices):
    barrier = pltpu.get_barrier_semaphore()
    for device in devices:
        pl.semaphore_signal(barrier, inc=1, device_id=device, device_id_type=MESH)
    pl.semaphore_wait(barrier, len(devices))


def tile_tables(tile, rand_ref, segq_ref, blocks):
    wide = NH * TILE
    key = lax.broadcasted_iota(jnp.int32, (blocks, wide), 0)
    lane = lax.broadcasted_iota(jnp.int32, (blocks, wide), 1)
    query = tile * (TILE // BLOCK) + lax.rem(lane, TILE) // BLOCK
    near = (key - query) * (key - query) <= 1
    hits = near.astype(F32)
    for r in range(rand_ref.shape[1]):
        hits = hits + (rand_ref[tile, r : r + 1, :] == key).astype(F32)
    fixed = jnp.logical_or(query < 2, key < 2)
    count = jnp.where(query < 2, 0.0, hits) + fixed.astype(F32)
    on = jnp.where(count > 0.0, jnp.log2(jnp.maximum(count, 1.0)), NEG)
    off = jnp.where(fixed, 0.0, NEG)
    return on, off, segq_ref[tile]


def biased(s, mask, on, off, first_block):
    rows = []
    for j in range(s.shape[0] // BLOCK):
        kb = first_block + j
        m3 = jnp.concatenate([mask[BLOCK * j : BLOCK * (j + 1)]] * NH, axis=1)
        bias = jnp.where(m3, on[kb : kb + 1, :], off[kb : kb + 1, :])
        rows.append(s[BLOCK * j : BLOCK * (j + 1)] * SCALE2 + bias)
    return jnp.concatenate(rows, axis=0)


def fill_segments(segq, segk):
    steps = segq.shape[0]
    for i in range(steps):
        column = jnp.broadcast_to(segq[i].astype(F32), (8, TILE)).T[:, :1]
        segk[TILE * i : TILE * (i + 1), :] = jnp.broadcast_to(column, (TILE, TILE)).astype(jnp.int32)


def forward_tile(tile, rand, segq, segk, qt, kn, vt, q3, tbuf, att, otile, lse):
    length = kn.shape[0]
    chunks = length // CH
    here = pl.ds(pl.multiple_of(tile * TILE, TILE), TILE)
    on, off, seg = tile_tables(tile, rand, segq, length // BLOCK)
    for h in range(NH):
        q3[HEAD * h : HEAD * (h + 1), TILE * h : TILE * (h + 1)] = qt[
            HEAD * h : HEAD * (h + 1), here
        ]
    top = jnp.full((8, NH * TILE), NEG, F32)
    for j in range(chunks):
        rows = slice(CH * j, CH * (j + 1))
        s = nn(kn[rows, :], q3[...])
        t = biased(s, segk[rows, :] == seg, on, off, CH // BLOCK * j)
        tbuf[rows, :] = t
        top = jnp.maximum(top, jnp.max(t.reshape(CH // 8, 8, NH * TILE), axis=0))
    peak = jnp.max(top, axis=0, keepdims=True)
    total = jnp.zeros((8, NH * TILE), F32)
    out = jnp.zeros((256, NH * TILE), F32)
    for j in range(chunks):
        rows = slice(CH * j, CH * (j + 1))
        p = jnp.exp2(tbuf[rows, :] - peak)
        total = total + jnp.sum(p.reshape(CH // 8, 8, NH * TILE), axis=0)
        out = out + nn(vt[:, rows], p.astype(BF16))
    weight = jnp.sum(total, axis=0, keepdims=True)
    lse[tile] = peak + jnp.log2(weight)
    inv = 1.0 / weight
    heads = [
        out[HEAD * h : HEAD * (h + 1), TILE * h : TILE * (h + 1)] * inv[:, TILE * h : TILE * (h + 1)]
        for h in range(NH)
    ]
    merged = jnp.concatenate(heads, axis=0)
    otile[tile] = merged
    att[here, :] = merged.T.astype(BF16)


def unit_place(me, u):
    low = lax.rem(me.z, 2)
    return 2 * lax.rem(me.half + 1 + u // 2, 2) + lax.rem(low + 1 + u, 2)


def forward_kernel(*refs):
    (x, wg, wo, wu, wd, rand, segq), refs = refs[:7], refs[7:]
    outs, refs = refs[:14], refs[14:]
    wof, wuf, wdf, att_out, otile_o, lse_o, segk_o, qn_o, kn_o, vn_o, qt_o, kt_o, xst_o, wgf_o = outs
    (xs, wgf, bo, bu, bd, att, home, otile, lse, segk), refs = refs[:10], refs[10:]
    (qn, kn, vn, qt, kt, vt, xst, q3, tbuf), refs = refs[:9], refs[9:]
    send, recv, xsend, xrecv, local = refs
    me = Place()
    d, t, c, z = me.d, me.t, me.c, me.z
    mine, other = me.half, 1 - me.half
    is_middle = z == 1 + me.half
    tok = x.shape[1]
    length = xs.shape[0]
    steps = length // TILE
    per_unit = 2 * tok // TILE
    loads = [
        pltpu.make_async_copy(src, dst, local.at[i])
        for i, (src, dst) in enumerate(((wo, bo), (wu, bu), (wd, bd)))
    ]
    for load in loads:
        load.start()
    meet([me.across_x, me.across_y] + [(d, lax.rem(t + k, 8)) for k in range(1, 8)])
    cps = Copies(send, recv)
    sent = []

    def begin(*copies):
        for cp in copies:
            cp.start()
            sent.append(cp)

    def rows_of(index):
        return pl.ds(pl.multiple_of(index * tok, tok), tok)

    shard = wg.shape[0]
    wrows = lambda index, start, size: pl.ds(pl.multiple_of(index * shard + start, size), size)
    wg_x = cps.to(wg, wgf.at[wrows(d, 0, shard)], me.across_x)
    wg_y = cps.to(wg, wgf.at[wrows(d, 0, shard)], me.across_y)
    near = cps.to(x.at[mine], xs.at[rows_of(t)], me.at_z(me.pair_z))
    give = cps.to(x.at[mine], xs.at[rows_of(t)], me.partner)
    far = pltpu.make_async_remote_copy(
        src_ref=x.at[other], dst_ref=xs.at[rows_of(t)], send_sem=xsend.at[0],
        recv_sem=xrecv.at[lax.rem(z, 2)], device_id=me.at_z(2 - me.half), device_id_type=MESH,
    )
    begin(wg_x, wg_y, far, near, give)
    heavy = []
    for w, full in ((wo, wof), (wu, wuf), (wd, wdf)):
        rows = w.shape[0] // 2
        part = pl.ds(pl.multiple_of(c * rows, rows), rows)
        to_x = cps.to(w.at[part], full.at[d, part], me.across_x)
        to_y = cps.to(w.at[part], full.at[d, part], me.across_y)
        begin(to_x, to_y)
        heavy.append((full, rows, part, to_x, to_y))

    xs[rows_of(t), :] = x[mine]
    wgf[wrows(d, 0, shard), :] = wg[...]
    q3[...] = jnp.zeros_like(q3)
    fill_segments(segq, segk)
    keeps = []
    for i, (load, buf, full) in enumerate(zip(loads, (bo, bu, bd), (wof, wuf, wdf))):
        load.wait()
        keep = pltpu.make_async_copy(buf, full.at[d], local.at[3 + i])
        keep.start()
        keeps.append(keep)

    half = shard // 2
    wg_x.wait_recv()
    lo = wrows(me.xn, 0, half)
    wg_dy = cps.to(wgf.at[lo], wgf.at[lo], me.across_y)
    begin(wg_dy)
    wg_y.wait_recv()
    hi = wrows(me.yn, half, half)
    wg_dx = cps.to(wgf.at[hi], wgf.at[hi], me.across_x)
    begin(wg_dx)

    def project(unit):
        rows = pl.ds(pl.multiple_of(unit * 2 * tok, 2 * tok), 2 * tok)
        both = nn(xs[rows, :], wgf[...])
        qf, kf, vf = both[:, :256], both[:, 256:512], both[:, 512:]
        qn[rows, :] = qf.astype(BF16)
        kn[rows, :] = kf.astype(BF16)
        vn[rows, :] = vf.astype(BF16)
        qt[:, rows] = qf.T.astype(BF16)
        kt[:, rows] = kf.T.astype(BF16)
        vt[:, rows] = vf.T.astype(BF16)
        xst[:, rows] = xs[rows, :].astype(F32).T.astype(BF16)

    wg_dy.wait_recv()
    wg_dx.wait_recv()
    give.wait_recv()
    near.wait_recv()
    near_rows = rows_of(2 * me.pair_z + c)
    pass_near = cps.to(xs.at[near_rows], xs.at[near_rows], me.partner)
    begin(pass_near)
    relays, onwards = [], []
    for j in range(2):
        src_rows = rows_of(2 * (2 * other + j) + c)
        relays.append(
            pltpu.make_async_remote_copy(
                src_ref=xs.at[src_rows], dst_ref=xs.at[src_rows], send_sem=xsend.at[1 + j],
                recv_sem=xrecv.at[j], device_id=me.at_z(me.pair_z), device_id_type=MESH,
            )
        )
        onwards.append(cps.to(xs.at[src_rows], xs.at[src_rows], me.partner))

    def forward_x(j):
        relays[j].wait_recv()
        pl.when(is_middle)(relays[j].start)
        begin(onwards[j])

    def arrive(k):
        if k == 0:
            forward_x(0)
        if k == 1:
            forward_x(1)
            pass_near.wait_recv()
        if k == 2:
            onwards[0].wait_recv()
        if k == 3:
            onwards[1].wait_recv()

    def project_step(k, carry):
        for i in range(4):
            pl.when(k == i)(functools.partial(arrive, i))
        unit = jnp.where(k < 2, 2 * mine + lax.rem(lax.rem(z, 2) + k, 2), 2 * other + k - 2)
        project(unit)
        return carry

    lax.fori_loop(0, 4, project_step, 0)
    saves = [
        pltpu.make_async_copy(src, dst, local.at[6 + i])
        for i, (src, dst) in enumerate(
            ((segk, segk_o), (qn, qn_o), (kn, kn_o), (vn, vn_o), (qt, qt_o), (kt, kt_o), (xst, xst_o), (wgf, wgf_o))
        )
    ]
    for save in saves:
        save.start()

    tail = []
    for full, rows, part, to_x, to_y in heavy:
        quarter = rows // 2
        lo = pl.ds(pl.multiple_of(c * rows, quarter), quarter)
        hi = pl.ds(pl.multiple_of(c * rows + quarter, quarter), quarter)
        tail.append(
            (
                to_x, to_y,
                cps.to(full.at[me.xn, lo], full.at[me.xn, lo], me.across_y),
                cps.to(full.at[me.xn, part], full.at[me.xn, part], me.partner),
                cps.to(full.at[me.yn, hi], full.at[me.yn, hi], me.across_x),
                cps.to(full.at[me.yn, part], full.at[me.yn, part], me.partner),
                cps.to(full.at[me.diag, part], full.at[me.diag, part], me.partner),
            )
        )

    def relay_weights(k):
        to_x, to_y, dy, px, dx, py, pd = tail[k]
        to_x.wait_recv()
        begin(dy, px)
        to_y.wait_recv()
        begin(dx, py)

    def relay_diag(k):
        to_x, to_y, dy, px, dx, py, pd = tail[k]
        dy.wait_recv()
        dx.wait_recv()
        begin(pd)

    homes = []
    for u in range(4):
        unit = unit_place(me, u)
        for o in range(1 if u == 3 else 0, 2):
            to = 2 * unit + (c if o == 0 else 1 - c)
            homes.append((u, cps.to(att.at[rows_of(to)], home.at[t], (d, to))))

    def send_home(u):
        for v, move in homes:
            if u == v:
                move.start()

    def between(i):
        if i == 0:
            relay_weights(0)
        if i == per_unit:
            send_home(0)
            relay_weights(1)
        if i == 2 * per_unit:
            send_home(1)
            relay_diag(0)
        if i == 3 * per_unit:
            send_home(2)
            relay_weights(2)
            relay_diag(1)

    def tile_step(i, carry):
        for point in range(0, steps, per_unit):
            pl.when(i == point)(functools.partial(between, point))
        tile = unit_place(me, i // per_unit) * per_unit + lax.rem(i, per_unit)
        forward_tile(tile, rand, segq, segk, qt, kn, vt, q3, tbuf, att, otile, lse)
        return carry

    lax.fori_loop(0, steps, tile_step, 0)
    send_home(3)
    last = [
        pltpu.make_async_copy(src, dst, local.at[14 + i])
        for i, (src, dst) in enumerate(((otile, otile_o), (lse, lse_o)))
    ]
    for save in last:
        save.start()
    home[t] = att[rows_of(t), :]
    relay_diag(2)
    for u, move in homes:
        move.wait()
    for s in range(2):
        pieces = [home[4 * s + g].astype(F32) for g in range(4)]
        att_out[tok * s : tok * (s + 1), :] = jnp.concatenate(pieces, axis=1).astype(BF16)
    for to_x, to_y, dy, px, dx, py, pd in tail:
        px.wait_recv()
        py.wait_recv()
        pd.wait_recv()
    for cp in sent:
        cp.wait_send()

    @pl.when(is_middle)
    def _():
        for relay in relays:
            relay.wait_send()

    for copy in keeps + saves + last:
        copy.wait()


def forward_half(x, wg, wo, wu, wd, rand, segq):
    dp = lax.axis_size("dp")
    seq = lax.axis_size("seq")
    tok, features = x.shape[1:]
    length = seq * tok
    steps = length // TILE
    nat, tra = (length, 256), (256, length)
    stacked = lambda w: jax.ShapeDtypeStruct((dp,) + w.shape, BF16)
    low = lambda *shape: jax.ShapeDtypeStruct(shape, BF16)
    full = lambda *shape: jax.ShapeDtypeStruct(shape, F32)
    return pl.pallas_call(
        forward_kernel,
        in_specs=[VMEMSPACE] * 2 + [ANYSPACE] * 3 + [VMEMSPACE] * 2,
        out_specs=[ANYSPACE] * 3 + [VMEMSPACE] + [ANYSPACE] * 10,
        out_shape=[
            stacked(wo), stacked(wu), stacked(wd), low(2 * tok, features),
            full(steps, NH * HEAD, TILE), full(steps, 1, NH * TILE),
            jax.ShapeDtypeStruct((length, TILE), jnp.int32),
            low(*nat), low(*nat), low(*nat), low(*tra), low(*tra),
            low(features, length), low(features, 768),
        ],
        scratch_shapes=[
            pltpu.VMEM((length, features), BF16),
            pltpu.VMEM((features, 768), BF16),
            pltpu.VMEM(wo.shape, BF16),
            pltpu.VMEM(wu.shape, BF16),
            pltpu.VMEM(wd.shape, BF16),
            pltpu.VMEM((length, NH * HEAD), BF16),
            pltpu.VMEM((seq, tok, NH * HEAD), BF16),
            pltpu.VMEM((steps, NH * HEAD, TILE), F32),
            pltpu.VMEM((steps, 1, NH * TILE), F32),
            pltpu.VMEM((length, TILE), jnp.int32),
            pltpu.VMEM(nat, BF16),
            pltpu.VMEM(nat, BF16),
            pltpu.VMEM(nat, BF16),
            pltpu.VMEM(tra, BF16),
            pltpu.VMEM(tra, BF16),
            pltpu.VMEM(tra, BF16),
            pltpu.VMEM((features, length), BF16),
            pltpu.VMEM((256, NH * TILE), BF16),
            pltpu.VMEM((length, NH * TILE), F32),
            pltpu.SemaphoreType.DMA((90,)),
            pltpu.SemaphoreType.DMA((90,)),
            pltpu.SemaphoreType.DMA((3,)),
            pltpu.SemaphoreType.DMA((2,)),
            pltpu.SemaphoreType.DMA((16,)),
        ],
        compiler_params=pltpu.CompilerParams(
            collective_id=0, has_side_effects=True, vmem_limit_bytes=62 * 1024 * 1024
        ),
        name="forward_half",
    )(x, wg, wo, wu, wd, rand, segq)


def each(count, body):
    def run(i, carry):
        body(i)
        return carry

    lax.fori_loop(0, count, run, 0)


def plus(a, b):
    return a.astype(F32) + b.astype(F32)


def backward_tile(
    tile, dat, qn, qt, otile, lse, rand, segq, segk, kn, vn, kt, dqkv, q3t, d3t, q3, d3, dk, dv
):
    chunks = kn.shape[0] // CH
    on, off, seg = tile_tables(tile, rand, segq, kn.shape[0] // BLOCK)
    here = pl.ds(pl.multiple_of(tile * TILE, TILE), TILE)
    dat_f = dat[here, :].astype(F32)
    dat_t = dat_f.T
    lane = lax.broadcasted_iota(jnp.int32, (TILE, NH * HEAD), 1) // HEAD
    qblk = qn[here, : NH * HEAD].astype(F32)
    delta = []
    for h in range(NH):
        hr = slice(HEAD * h, HEAD * (h + 1))
        hc = slice(TILE * h, TILE * (h + 1))
        q3t[hr, hc] = qt[hr, here]
        d3t[hr, hc] = dat_t[hr].astype(BF16)
        q3[hc, :] = jnp.where(lane == h, qblk, 0.0).astype(BF16)
        d3[hc, :] = jnp.where(lane == h, dat_f, 0.0).astype(BF16)
        delta.append(jnp.sum(dat_t[hr] * otile[tile, hr, :], axis=0, keepdims=True))
    delta = jnp.concatenate(delta, axis=1)
    norm = lse[tile]
    dq = jnp.zeros((256, NH * TILE), F32)
    for j in range(chunks):
        rows = slice(CH * j, CH * (j + 1))
        s = nn(kn[rows, :], q3t[...])
        dp = nn(vn[rows, :], d3t[...])
        t = biased(s, segk[rows, :] == seg, on, off, CH // BLOCK * j)
        p = jnp.exp2(t - norm)
        ds = (p * (dp - delta)).astype(BF16)
        dv[rows, :] += nn(p.astype(BF16), d3[...])
        dk[rows, :] += nn(ds, q3[...])
        dq = dq + nn(kt[:, rows], ds)
    heads = [dq[HEAD * h : HEAD * (h + 1), TILE * h : TILE * (h + 1)] for h in range(NH)]
    merged = jnp.concatenate(heads, axis=0).T * HEAD ** (-0.5)
    dqkv[here, : NH * HEAD] = merged.astype(BF16)


def backward_kernel(*refs):
    (src, stats, g0, g1, g2), refs = refs[:5], refs[5:]
    (rand, segq), refs = refs[:2], refs[2:]
    saved, refs = refs[:10], refs[10:]
    (o0, o1, o2, stats_out, ig, wq), refs = refs[:6], refs[6:]
    bufs, refs = refs[:18], refs[18:]
    held, refs = refs[:10], refs[10:]
    kn, vn, kt, segk, qn, qt, otile, lse, xst, wg = held
    (dat, dqkv, q3t, d3t, q3, d3, dk, dv), refs = refs[:8], refs[8:]
    (part, own_p, rp, ra_p, rb_p, ro, dwg, wb1, wb2, wc, wr), refs = refs[:11], refs[11:]
    nsend, nrecv, send, recv, local = refs
    me = Place()
    c, z, x, y, t = me.c, me.z, me.x, me.y, me.t
    mine, other = me.half, 1 - me.half
    is_middle = z == 1 + me.half
    is_outer = z != 1 + me.half
    z_step = [lax.rem(z + k, 4) for k in (1, 2, 3)]
    tok = src.shape[1]
    loads = [
        pltpu.make_async_copy(from_hbm, to_vmem, local.at[4 + i])
        for i, (from_hbm, to_vmem) in enumerate(zip(saved, held))
    ]
    for load in loads:
        load.start()
    meet([me.across_x, me.across_y] + [(me.d, lax.rem(t + k, 8)) for k in range(1, 8)])
    cps = Copies(send, recv)

    def rows_of(index):
        return pl.ds(pl.multiple_of(index * tok, tok), tok)

    dat_moves = []
    for u in range(4):
        place = unit_place(me, 3 - u)
        for o in range(1 if u == 0 else 0, 2):
            to = 2 * place + (c if o == 0 else 1 - c)
            dat_moves.append((u, cps.to(src.at[to], dat.at[rows_of(t)], (me.d, to))))
    for u, move in dat_moves:
        move.start()
    keep = pltpu.make_async_copy(src.at[t], dat.at[rows_of(t)], local.at[3])
    keep.start()

    works = []
    for i, (g, o) in enumerate(((g2, o2), (g1, o1), (g0, o0))):
        own, ra, rb1, rb2, rc, rd = bufs[6 * i : 6 * i + 6]
        swap_core = cps.to(g.at[:, :, :, 1 - c], ra, me.partner)
        swap_core.start()
        load = pltpu.make_async_copy(g.at[:, :, :, c], own, local.at[i])
        load.start()
        moves = (
            swap_core,
            load,
            cps.to(own.at[:, 1 - x, 0:2], rb1, me.across_x),
            cps.to(own.at[1 - y, :, 2:4], rb2, me.across_y),
            cps.to(rb1.at[1 - y], rc.at[0:2], me.across_y),
            cps.to(rb2.at[1 - x], rc.at[2:4], me.across_x),
            [cps.to(rc.at[k], rd.at[j], me.at_z(k)) for j, k in enumerate(z_step)],
        )
        works.append(((o, own, ra, rb1, rb2, rc, rd), moves))
    stat_to = [me.partner, me.across_x, me.across_y, me.at_z(me.pair_z), me.at_z(lax.rem(z + 2, 4))]
    stat_all = [cps.to(nsend.at[k], nrecv.at[k], stat_to[k]) for k in range(5)]

    def stat_step(k):
        if k == 0:
            nsend[0] = stats[...]
        else:
            stat_all[k - 1].wait_recv()
            nsend[k] = nsend[k - 1] + nrecv[k - 1]
        stat_all[k].start()

    sent = []

    def begin(*copies):
        for cp in copies:
            cp.start()
            sent.append(cp)

    def stage_a(work):
        (o, own, ra, rb1, rb2, rc, rd), (swap_core, load, bx, by, cy, cx, ds) = work
        load.wait()
        swap_core.wait_recv()

        def fold(i):
            yy, xx, zz = i // 8, lax.rem(i // 4, 2), lax.rem(i, 4)
            own[yy, xx, zz] = plus(own[yy, xx, zz], ra[yy, xx, zz]).astype(BF16)

        each(16, fold)
        begin(bx, by)

    def stage_b(work):
        (o, own, ra, rb1, rb2, rc, rd), (swap_core, load, bx, by, cy, cx, ds) = work
        bx.wait_recv()

        def fold_x(i):
            yy, zz = i // 2, lax.rem(i, 2)
            rb1[yy, zz] = plus(own[yy, x, zz], rb1[yy, zz]).astype(BF16)

        each(4, fold_x)
        begin(cy)
        by.wait_recv()

        def fold_y(i):
            xx, zz = i // 2, lax.rem(i, 2)
            rb2[xx, zz] = plus(own[y, xx, 2 + zz], rb2[xx, zz]).astype(BF16)

        each(4, fold_y)
        begin(cx)

    def stage_c(work):
        (o, own, ra, rb1, rb2, rc, rd), (swap_core, load, bx, by, cy, cx, ds) = work
        cy.wait_recv()
        cx.wait_recv()
        for zz in range(2):
            rc[zz] = plus(rb1[y, zz], rc[zz]).astype(BF16)
            rc[2 + zz] = plus(rb2[x, zz], rc[2 + zz]).astype(BF16)
        begin(*ds)

    def stage_d(work):
        (o, own, ra, rb1, rb2, rc, rd), (swap_core, load, bx, by, cy, cx, ds) = work
        for cp in ds:
            cp.wait_recv()
        o[...] = plus(rc[z], rd[0]) + plus(rd[1], rd[2])

    q3t[...] = jnp.zeros_like(q3t)
    d3t[...] = jnp.zeros_like(d3t)
    dk[...] = jnp.zeros_like(dk)
    dv[...] = jnp.zeros_like(dv)
    gap = jnp.zeros((dqkv.shape[0], 256 - NH * HEAD), BF16)
    for g in range(3):
        dqkv[:, 256 * g + NH * HEAD : 256 * (g + 1)] = gap
    stat_step(0)
    for load in loads[:8]:
        load.wait()
    keep.wait()
    per_unit = 2 * tok // TILE
    steps = dqkv.shape[0] // TILE

    def before_unit(u):
        for v, move in dat_moves:
            if u == v:
                move.wait_recv()
        if u == 1:
            for work in works:
                stage_a(work)
            stat_step(1)
        if u == 2:
            stat_step(2)
        if u == 3:
            stage_b(works[0])
            stat_step(3)

    def tile_step(i, carry):
        for u in range(4):
            pl.when(i == u * per_unit)(functools.partial(before_unit, u))
        tile = unit_place(me, 3 - i // per_unit) * per_unit + lax.rem(i, per_unit)
        backward_tile(
            tile, dat, qn, qt, otile, lse, rand, segq, segk, kn, vn, kt, dqkv,
            q3t, d3t, q3, d3, dk, dv,
        )
        return carry

    lax.fori_loop(0, steps, tile_step, 0)
    stage_b(works[1])
    stage_b(works[2])
    stat_step(4)
    loads[9].wait()

    dqkv[:, 256 : 256 + NH * HEAD] = (dk[...] * HEAD ** (-0.5)).astype(BF16)
    dqkv[:, 512 : 512 + NH * HEAD] = dv[...].astype(BF16)
    order = [2 * other, 2 * other + 1, me.pair_z, z]
    cores = []
    for zz in order:
        rows = pl.ds(pl.multiple_of(zz * 2 * tok, 2 * tok), 2 * tok)
        grad = nt(dqkv[rows, :], wg[...]).astype(BF16)
        part[zz, 0] = grad[:tok]
        part[zz, 1] = grad[tok:]
        core = cps.to(part.at[zz, 1 - c], rp.at[zz], me.partner)
        begin(core)
        cores.append(core)
    stage_c(works[0])

    up = [cps.to(own_p.at[2 * other + j], rb_p.at[j], me.at_z(me.pair_z)) for j in range(2)]
    near = cps.to(own_p.at[me.pair_z], ra_p, me.at_z(me.pair_z))
    for k, zz in enumerate(order):
        cores[k].wait_recv()
        own_p[zz] = plus(part[zz, c], rp[zz]).astype(BF16)
        if k < 2:
            pl.when(is_outer)(up[k].start)
        if k == 2:
            begin(near)
    loads[8].wait()
    half_rows = xst.shape[0] // 2
    for yy in range(2):
        grad = nn(xst[half_rows * yy : half_rows * (yy + 1), :], dqkv[...]).astype(BF16)
        dwg[yy] = grad.reshape(dwg.shape[1:])
    bx = cps.to(dwg.at[:, 1 - x, 0:4], wb1, me.across_x)
    by = cps.to(dwg.at[1 - y, :, 4:8], wb2, me.across_y)
    begin(bx, by)
    down_send, down_recv = cps.used, cps.used
    cps.used += 2
    down = [
        pltpu.make_async_remote_copy(
            src_ref=own_p.at[2 * other + j], dst_ref=ro, send_sem=send.at[down_send + j],
            recv_sem=recv.at[down_recv], device_id=me.at_z(2 * other + j), device_id_type=MESH,
        )
        for j in range(2)
    ]

    @pl.when(is_middle)
    def _():
        for j in range(2):
            up[j].wait_recv()
            own_p[2 * other + j] = plus(own_p[2 * other + j], rb_p[j]).astype(BF16)
            down[j].start()

    stage_c(works[1])
    stage_c(works[2])
    bx.wait_recv()

    def fold_x(i):
        yy, tt = i // 4, lax.rem(i, 4)
        wb1[yy, tt] = plus(dwg[yy, x, tt], wb1[yy, tt]).astype(BF16)

    each(8, fold_x)
    cy = cps.to(wb1.at[1 - y], wc.at[0:4], me.across_y)
    begin(cy)
    by.wait_recv()

    def fold_y(i):
        xx, tt = i // 4, lax.rem(i, 4)
        wb2[xx, tt] = plus(dwg[y, xx, 4 + tt], wb2[xx, tt]).astype(BF16)

    each(8, fold_y)
    cx = cps.to(wb2.at[1 - x], wc.at[4:8], me.across_x)
    begin(cx)
    stat_all[-1].wait_recv()
    stats_out[...] = nsend[4] + nrecv[4]
    cy.wait_recv()
    cx.wait_recv()

    def fold_c(i):
        wc[i] = plus(wb1[y, i], wc[i]).astype(BF16)
        wc[4 + i] = plus(wb2[x, i], wc[4 + i]).astype(BF16)

    each(4, fold_c)
    moves = []
    for k in range(1, 8):
        peer = lax.rem(t + k, 8)
        moves.append(cps.to(wc.at[peer], wr.at[t], (me.d, peer)))
    begin(*moves)
    near.wait_recv()
    ig[mine] = plus(own_p[z], ra_p[...])
    down[0].wait_recv()
    ig[other] = ro[...].astype(F32)
    for work in works:
        stage_d(work)
    wr[t] = wc[t]
    for move in moves:
        move.wait_recv()
    for g in range(4):
        wq[g] = plus(wr[g], wr[4 + g])
    for cp in sent + stat_all + [move for u, move in dat_moves] + [moves[0] for refs, moves in works]:
        cp.wait_send()

    @pl.when(is_outer)
    def _():
        for cp in up:
            cp.wait_send()

    @pl.when(is_middle)
    def _():
        for cp in down:
            cp.wait_send()


def backward_half(src, stats, grads, rand, segq, saved):
    dims = [g.shape[-2:] for g in grads]
    tok = src.shape[1]
    features, length = saved[8].shape
    bufs = []
    for rows, cols in dims[::-1]:
        bufs += [
            pltpu.VMEM((2, 2, 4, rows, cols), BF16),
            pltpu.VMEM((2, 2, 4, rows, cols), BF16),
            pltpu.VMEM((2, 2, rows, cols), BF16),
            pltpu.VMEM((2, 2, rows, cols), BF16),
            pltpu.VMEM((4, rows, cols), BF16),
            pltpu.VMEM((3, rows, cols), BF16),
        ]
    wrows = features // 32
    return pl.pallas_call(
        backward_kernel,
        in_specs=[VMEMSPACE] * 2 + [ANYSPACE] * 3 + [VMEMSPACE] * 2 + [ANYSPACE] * 10,
        out_specs=[VMEMSPACE] * 6,
        out_shape=[jax.ShapeDtypeStruct(dim, F32) for dim in dims]
        + [
            jax.ShapeDtypeStruct(stats.shape, F32),
            jax.ShapeDtypeStruct((2, tok, features), F32),
            jax.ShapeDtypeStruct((4, wrows, 768), F32),
        ],
        scratch_shapes=bufs
        + [pltpu.VMEM(a.shape, a.dtype) for a in saved]
        + [
            pltpu.VMEM((length, NH * HEAD), BF16),
            pltpu.VMEM((length, 768), BF16),
            pltpu.VMEM((256, NH * TILE), BF16),
            pltpu.VMEM((256, NH * TILE), BF16),
            pltpu.VMEM((NH * TILE, NH * HEAD), BF16),
            pltpu.VMEM((NH * TILE, NH * HEAD), BF16),
            pltpu.VMEM((length, NH * HEAD), F32),
            pltpu.VMEM((length, NH * HEAD), F32),
            pltpu.VMEM((4, 2, tok, features), BF16),
            pltpu.VMEM((4, tok, features), BF16),
            pltpu.VMEM((4, tok, features), BF16),
            pltpu.VMEM((tok, features), BF16),
            pltpu.VMEM((2, tok, features), BF16),
            pltpu.VMEM((tok, features), BF16),
            pltpu.VMEM((2, 2, 8, wrows, 768), BF16),
            pltpu.VMEM((2, 4, wrows, 768), BF16),
            pltpu.VMEM((2, 4, wrows, 768), BF16),
            pltpu.VMEM((8, wrows, 768), BF16),
            pltpu.VMEM((8, wrows, 768), BF16),
            pltpu.VMEM((5,) + stats.shape, F32),
            pltpu.VMEM((5,) + stats.shape, F32),
            pltpu.SemaphoreType.DMA((90,)),
            pltpu.SemaphoreType.DMA((90,)),
            pltpu.SemaphoreType.DMA((14,)),
        ],
        compiler_params=pltpu.CompilerParams(
            collective_id=3, has_side_effects=True, vmem_limit_bytes=62 * 1024 * 1024
        ),
        name="backward_half",
    )(src, stats, *grads, rand, segq, *saved)


def head_layout(
    inputs, segments, rand_blocks, w_qkv, w_out, w_up, w_down, norm_gain, norm_bias, out_grad
):
    seqs, tok, features = inputs.shape
    seq = lax.axis_size("seq")
    t = lax.axis_index("seq")
    groups = seq // seqs
    my_seq, my_group = t // groups, lax.rem(t, groups)
    width = features // groups
    shard = w_qkv.reshape(w_qkv.shape[0], 3, groups, width)
    shard = lax.dynamic_index_in_dim(shard, my_group, 2, keepdims=False)
    shard = jnp.pad(shard, ((0, 0), (0, 0), (0, 256 - width))).reshape(w_qkv.shape[0], 768)
    steps = seq * tok // TILE
    rand = lax.dynamic_slice_in_dim(
        lax.dynamic_index_in_dim(rand_blocks, my_seq, 0, keepdims=False), my_group * NH, NH, 1
    )
    rand = rand.reshape(steps, TILE // BLOCK, NH, 3).transpose(0, 3, 2, 1)
    rand = jnp.broadcast_to(rand[..., None], rand.shape + (BLOCK,)).reshape(steps, 3, NH * TILE)
    seg = lax.dynamic_index_in_dim(segments, my_seq, 0, keepdims=False)
    segq = seg.reshape(steps, 1, TILE)
    wof, wuf, wdf, att_flat, otile, lse, segk, qn, kn, vn, qt, kt, xst, wgf = forward_half(
        inputs, shard, w_out, w_up, w_down, rand, segq
    )
    full_out = wof.reshape(features, features)
    full_up = wuf.reshape(features, -1)
    full_down = wdf.reshape(-1, features)
    tokens_flat = inputs.reshape(seqs * tok, features)
    resid_one = tokens_flat.astype(F32) + product(att_flat, full_out)
    hidden_one, normed_one, inv_one = norm_forward(resid_one, norm_gain[0], norm_bias[0])
    hidden_low = hidden_one.astype(BF16)
    pre_act = product(hidden_low, full_up)
    activated = gelu_value(pre_act).astype(BF16)
    resid_two = hidden_one + product(activated, full_down)
    result, normed_two, inv_two = norm_forward(resid_two, norm_gain[1], norm_bias[1])
    grad_rows = out_grad.reshape(seqs * tok, features).astype(F32)
    grad_resid_two, gain_two, shift_two = norm_backward(
        grad_rows, normed_two, inv_two, norm_gain[1]
    )
    grad_branch = grad_resid_two.astype(BF16)
    grad_down_w = product_tn(activated, grad_branch).astype(BF16)
    grad_pre = (product_nt(grad_branch, full_down) * gelu_slope(pre_act)).astype(BF16)
    grad_up_w = product_tn(hidden_low, grad_pre).astype(BF16)
    grad_hidden = grad_resid_two + product_nt(grad_pre, full_up)
    grad_resid_one, gain_one, shift_one = norm_backward(
        grad_hidden, normed_one, inv_one, norm_gain[0]
    )
    grad_mix = grad_resid_one.astype(BF16)
    grad_out_w = product_tn(att_flat, grad_mix).astype(BF16)
    grad_att = product_nt(grad_mix, full_out).astype(BF16)
    grad_att = grad_att.reshape(seqs, tok, groups, width).transpose(0, 2, 1, 3)
    src = grad_att.reshape(seq, tok, width)
    stats = jnp.stack([gain_one, gain_two, shift_one, shift_two])
    cut = lambda g: g.reshape(2, 2, 4, 2, g.shape[0] // 32, g.shape[1])
    out_sum, up_sum, down_sum, stats, ig, wq = backward_half(
        src, stats, [cut(grad_out_w), cut(grad_up_w), cut(grad_down_w)], rand, segq,
        (kn, vn, kt, segk, qn, qt, otile, lse, xst, wgf),
    )
    wq = wq.reshape(groups, features // 32, 3, 256)[..., :width].transpose(1, 2, 0, 3)
    mine = lax.axis_index("dp") * seq + t
    stats = lax.dynamic_slice_in_dim(stats, mine * (features // 32), features // 32, 1)
    return (
        result.astype(BF16).reshape(seqs, tok, features),
        ig + grad_resid_one.reshape(seqs, tok, features),
        wq.reshape(features // 32, 3 * features),
        out_sum,
        up_sum,
        down_sum,
        stats[:2],
        stats[2:],
    )


def solution(mesh):
    in_specs = (
        P("dp", "seq", None),
        P("dp", None),
        P("dp", None, None, None),
        P("dp", None),
        P("dp", None),
        P("dp", None),
        P("dp", None),
        P(),
        P(),
        P("dp", "seq", None),
    )
    out_specs = (
        P("dp", "seq", None),
        P("dp", "seq", None),
        P(("dp", "seq"), None),
        P(("dp", "seq"), None),
        P(("dp", "seq"), None),
        P(("dp", "seq"), None),
        P(None, ("dp", "seq")),
        P(None, ("dp", "seq")),
    )
    fits = mesh.shape["dp"] == 4 and mesh.shape["seq"] == 8
    return jax.shard_map(
        head_layout if fits else per_device, mesh=mesh, in_specs=in_specs, out_specs=out_specs, check_vma=False
    )
```

profile of v0, /device:TPU:0, one launch (start us, length us, event | category | flops | bytes accessed | tf_op | source)
XLA Modules:
  0.0 261.3 jit_solution(14398225087915748777)
XLA Ops:
  0.6 0.0 copy-start
  0.7 0.7 copy-done
  1.4 1.3 dynamic-slice_bitcast_fusion.refs_6_
  2.7 0.8 slice_reduce_fusion
  3.5 1.4 convert_reduce_fusion
  5.0 0.1 div.42
  5.1 0.1 copy.26
  5.1 0.4 copy.27
  5.5 0.2 broadcast_in_dim.2
  5.7 0.8 reshape.131.refs_5_
  6.5 1.1 reshape.128
  7.6 0.6 constant_dynamic-slice_fusion.2
  8.3 0.3 copy.30
  8.5 0.2 pad.4.clone
  8.7 0.8 copy.31
  9.5 91.8 %forward_half.1 = (bf16[4,192,768]{2,1,0:T(8,128)(2,1)}, bf16[4,192,3072]{2,1,0:T(8,128)(2,1)}, bf16[4,768,768]{2,1,0:T(8,128)(2,1)}, bf16[384,768]{1,0:T(8,128)...) custom-call(bf16[2,192,768]{2,1,0:T(8,128)(2,1)} %refs_0_.1, ...), custom_call_target="tpu_custom_call" | custom-call | tf_op jit(solution)/shard_map/forward_half/pallas_call | solution.py:892
  101.3 2.3 fusion.22
  103.7 0.3 multiply_reduce_fusion.3
  103.9 0.3 copy-done.12
  104.2 2.4 multiply_convert_fusion
  106.7 2.2 fusion.23
  108.9 0.3 multiply_reduce_fusion.2
  109.1 0.8 copy-done.1
  109.9 0.6 fusion.12
  110.5 1.3 fusion.9
  111.8 3.4 %fusion.5 = bf16[384,3072]{1,0:T(8,128)(2,1)S(1)} fusion(f32[384,3072]{1,0:T(8,128)S(1)} %get-tuple-element.67, bf16[3072,768]{1,0:T(8,128)(2,1)S(1)} %bitcast.70, f32[384,768]{1,0:T(8,128)S(1)} %get-tuple-element.60), kind=kOutput, calls=%fused_computation.8 | convolution fusion | flops 1824030720 | bytes 12976128 | tf_op jit(solution)/shard_map/dot_general | solution.py:66
  115.2 2.4 multiply_reduce_fusion
  117.6 0.4 subtract_multiply_fusion
  118.0 0.9 copy-done.2
  118.9 1.5 convolution_convert_fusion.3
  120.4 0.6 pad_maximum_fusion.refs_1_
  121.0 2.3 reshape.137
  123.3 1.0 copy.28
  124.3 0.2 copy-done.4
  124.5 1.8 convolution_convert_fusion.2
  126.3 4.7 %convolution_convert_fusion.1 = bf16[768,3072]{1,0:T(8,128)(2,1)} fusion(bf16[384,3072]{1,0:T(8,128)(2,1)S(1)} %copy-done.16, f32[384,768]{1,0:T(8,128)S(1)} %get-tuple-element.65, f32[768]{0:T(1024)S(1)} %get-tuple-element.59, f32[768]{0:T(1024)S(1)} %get-tuple-element.71, f32[384]{0:T(512)S(1)} %add_rsqrt_fusion.1, f32[384]{0:T(512)S(1)} %broadcast_multiply_fusion.5), kind=kOutput, calls=%fused_computation.2 | convolution fusion | flops 1815773184 | bytes 8266752 | tf_op jit(solution)/shard_map/dot_general | solution.py:60
  131.0 4.3 %convolution_convert_fusion = bf16[3072,768]{1,0:T(8,128)(2,1)} fusion(bf16[384,3072]{1,0:T(8,128)(2,1)S(1)} %copy-done.14, f32[384,768]{1,0:T(8,128)S(1)} %copy-done.6), kind=kOutput, calls=%fused_computation.1 | convolution fusion | flops 1814593536 | bytes 8257536 | tf_op jit(solution)/shard_map/dot_general | solution.py:60
  135.3 118.7 %backward_half.1 = (f32[24,768]{1,0:T(8,128)}, f32[24,3072]{1,0:T(8,128)}, f32[96,768]{1,0:T(8,128)}, f32[4,768]{1,0:T(4,128)}, f32[2,192,768]{2,1,0:T(8,128)}, /*index=5*/f32[4,24,768]{2,1,0:T(8,128)}) custom-call(bf16[8,192,192]{2,1,0:T(8,128)(2,1)} %bitcast.58, f32[4,768]{1,0:T(4,128)} %pad_maximum_fusion.refs_1_, ...), custom_call_target="tpu_custom_call" | custom-call | tf_op jit(solution)/shard_map/backward_half/pallas_call | solution.py:1274
  254.0 2.6 add.97
  256.6 0.8 constant_dynamic-slice_fusion
  257.3 0.6 fusion.21
  257.9 0.2 reshape.143
  258.1 0.1 slice_bitcast_fusion
  258.2 0.2 copy.29
  258.4 0.9 reshape.144
  259.3 0.6 copy.37
  259.9 0.7 copy.38
  260.6 0.7 copy.39
  (47 shorter events, 0.2 us)
Async XLA Ops:
  0.6 0.8 copy-start
  0.6 5.9 %copy-start.7 = (bf16[192,2304]{1,0:T(8,128)(2,1)S(1)}, bf16[192,2304]{1,0:T(8,128)(2,1)}, u32[]{:S(2)}) copy-start(bf16[192,2304]{1,0:T(8,128)(2,1)} %param.13) | copy-start | bytes 2654212
  9.5 91.8 %copy-start.3 = (bf16[2,192,768]{2,1,0:T(8,128)(2,1)S(1)}, bf16[2,192,768]{2,1,0:T(8,128)(2,1)}, u32[]{:S(2)}) copy-start(bf16[2,192,768]{2,1,0:T(8,128)(2,1)} %refs_0_.1) | copy-start | bytes 1769476
  101.3 2.9 %copy-start.12 = (bf16[4,192,3072]{2,1,0:T(8,128)(2,1)S(1)}, bf16[4,192,3072]{2,1,0:T(8,128)(2,1)}, u32[]{:S(2)}) copy-start(bf16[4,192,3072]{2,1,0:T(8,128)(2,1)} %get-tuple-element.30) | copy-start | bytes 14155780
  103.7 3.0 %slice-start = ((s8[4718592]{0:T(1024)(128)(4,1)}), s8[4194304]{0:T(1024)(128)(4,1)S(1)}, s32[]{:S(2)}) async-start(s8[4718592]{0:T(1024)(128)(4,1)} %bitcast.67), calls=%async_computation | async-start | bytes 8388608
  104.2 2.5 slice-start.1
  106.7 2.2 copy-start.13
  108.9 1.1 copy-start.1
  111.8 3.4 %copy-start.5 = (f32[384,768]{1,0:T(8,128)}, f32[384,768]{1,0:T(8,128)S(1)}, u32[]{:S(2)}) copy-start(f32[384,768]{1,0:T(8,128)S(1)} %get-tuple-element.60) | copy-start | bytes 3538948
  115.2 2.4 copy-start.15
  117.6 1.3 copy-start.2
  123.3 1.2 copy-start.4
  124.5 1.8 copy-start.16
  126.3 4.7 %copy-start.6 = (f32[384,768]{1,0:T(8,128)S(1)}, f32[384,768]{1,0:T(8,128)}, u32[]{:S(2)}) copy-start(f32[384,768]{1,0:T(8,128)} %copy-done.5) | copy-start | bytes 3538948
  126.3 4.7 %copy-start.14 = (bf16[384,3072]{1,0:T(8,128)(2,1)S(1)}, bf16[384,3072]{1,0:T(8,128)(2,1)}, u32[]{:S(2)}) copy-start(bf16[384,3072]{1,0:T(8,128)(2,1)} %copy-done.13) | copy-start | bytes 7077892
  254.0 3.9 %copy-start.10 = (f32[4,24,768]{2,1,0:T(8,128)S(1)}, f32[4,24,768]{2,1,0:T(8,128)}, u32[]{:S(2)}) copy-start(f32[4,24,768]{2,1,0:T(8,128)} %get-tuple-element.43) | copy-start | bytes 884740
  257.9 1.3 copy-start.11
  258.1 1.8 copy-start.9
  258.1 2.5 copy-start.8
where the time goes:
time: 262 us; the launch traced here: 261 us
  Pallas kernels  211 us (81%)
  matrix products  25 us (10%)
  local copies, waits for them, and re-layouts  17.4 us (7%)
  other arithmetic  7.36 us (3%)
    pallas_call x1, Pallas kernels, backward_half(): pl.pallas_call(backward_kernel, in_specs=[VMEMSPACE] * 2 + [ANYSPACE] * 3...  119 us
    pallas_call x1, Pallas kernels, forward_half(): pl.pallas_call(forward_kernel, in_specs=[VMEMSPACE] * 2 + [ANYSPACE] * 3...  91.8 us
    dot_general x3, matrix products, product_tn(): lax.dot_general(left_side, right_side, (((0,), (0,)), ((), ())), preferre...  10.9 us
    dot_general x3, matrix products, product_nt(): lax.dot_general(left_side, right_side, (((1,), (1,)), ((), ())), preferre...  7.26 us
    dot_general x3, matrix products, product(): return jnp.dot(left_side, right_side, preferred_element_type=jnp.float32)  6.91 us
    unnamed x43, local copies, waits for them, and re-layouts  5.95 us

commit v1 on v0

--- a/solution.py
+++ b/solution.py
@@ -684,23 +684,36 @@
 
     shard = wg.shape[0]
     wrows = lambda index, start, size: pl.ds(pl.multiple_of(index * shard + start, size), size)
-    wg_x = cps.to(wg, wgf.at[wrows(d, 0, shard)], me.across_x)
-    wg_y = cps.to(wg, wgf.at[wrows(d, 0, shard)], me.across_y)
+    half = shard // 2
+    top_half, low_half = pl.ds(0, half), pl.ds(half, half)
+    my_top, my_low = wrows(d, 0, half), wrows(d, half, half)
+    wg_x0 = cps.to(wg.at[top_half], wgf.at[my_top], me.across_x)
+    wg_x1 = cps.to(wg.at[low_half], wgf.at[my_low], me.across_x)
+    wg_y0 = cps.to(wg.at[low_half], wgf.at[my_low], me.across_y)
+    wg_y1 = cps.to(wg.at[top_half], wgf.at[my_top], me.across_y)
     near = cps.to(x.at[mine], xs.at[rows_of(t)], me.at_z(me.pair_z))
     give = cps.to(x.at[mine], xs.at[rows_of(t)], me.partner)
     far = pltpu.make_async_remote_copy(
         src_ref=x.at[other], dst_ref=xs.at[rows_of(t)], send_sem=xsend.at[0],
         recv_sem=xrecv.at[lax.rem(z, 2)], device_id=me.at_z(2 - me.half), device_id_type=MESH,
     )
-    begin(wg_x, wg_y, far, near, give)
+    begin(wg_x0, wg_y0, far, wg_x1, wg_y1, near, give)
     heavy = []
     for w, full in ((wo, wof), (wu, wuf), (wd, wdf)):
         rows = w.shape[0] // 2
         part = pl.ds(pl.multiple_of(c * rows, rows), rows)
         to_x = cps.to(w.at[part], full.at[d, part], me.across_x)
         to_y = cps.to(w.at[part], full.at[d, part], me.across_y)
+        heavy.append((full, rows, part, to_x, to_y))
+    xn_top, yn_low = wrows(me.xn, 0, half), wrows(me.yn, half, half)
+    wg_dy = cps.to(wgf.at[xn_top], wgf.at[xn_top], me.across_y)
+    wg_dx = cps.to(wgf.at[yn_low], wgf.at[yn_low], me.across_x)
+    wg_x0.wait_recv()
+    begin(wg_dy)
+    wg_y0.wait_recv()
+    begin(wg_dx)
+    for full, rows, part, to_x, to_y in heavy[:2]:
         begin(to_x, to_y)
-        heavy.append((full, rows, part, to_x, to_y))
 
     xs[rows_of(t), :] = x[mine]
     wgf[wrows(d, 0, shard), :] = wg[...]
@@ -712,16 +725,6 @@
         keep = pltpu.make_async_copy(buf, full.at[d], local.at[3 + i])
         keep.start()
         keeps.append(keep)
-
-    half = shard // 2
-    wg_x.wait_recv()
-    lo = wrows(me.xn, 0, half)
-    wg_dy = cps.to(wgf.at[lo], wgf.at[lo], me.across_y)
-    begin(wg_dy)
-    wg_y.wait_recv()
-    hi = wrows(me.yn, half, half)
-    wg_dx = cps.to(wgf.at[hi], wgf.at[hi], me.across_x)
-    begin(wg_dx)
 
     def project(unit):
         rows = pl.ds(pl.multiple_of(unit * 2 * tok, 2 * tok), 2 * tok)
@@ -735,6 +738,8 @@
         vt[:, rows] = vf.T.astype(BF16)
         xst[:, rows] = xs[rows, :].astype(F32).T.astype(BF16)
 
+    wg_x1.wait_recv()
+    wg_y1.wait_recv()
     wg_dy.wait_recv()
     wg_dx.wait_recv()
     give.wait_recv()
@@ -758,34 +763,6 @@
         pl.when(is_middle)(relays[j].start)
         begin(onwards[j])
 
-    def arrive(k):
-        if k == 0:
-            forward_x(0)
-        if k == 1:
-            forward_x(1)
-            pass_near.wait_recv()
-        if k == 2:
-            onwards[0].wait_recv()
-        if k == 3:
-            onwards[1].wait_recv()
-
-    def project_step(k, carry):
-        for i in range(4):
-            pl.when(k == i)(functools.partial(arrive, i))
-        unit = jnp.where(k < 2, 2 * mine + lax.rem(lax.rem(z, 2) + k, 2), 2 * other + k - 2)
-        project(unit)
-        return carry
-
-    lax.fori_loop(0, 4, project_step, 0)
-    saves = [
-        pltpu.make_async_copy(src, dst, local.at[6 + i])
-        for i, (src, dst) in enumerate(
-            ((segk, segk_o), (qn, qn_o), (kn, kn_o), (vn, vn_o), (qt, qt_o), (kt, kt_o), (xst, xst_o), (wgf, wgf_o))
-        )
-    ]
-    for save in saves:
-        save.start()
-
     tail = []
     for full, rows, part, to_x, to_y in heavy:
         quarter = rows // 2
@@ -815,6 +792,36 @@
         dx.wait_recv()
         begin(pd)
 
+    def arrive(k):
+        if k == 0:
+            forward_x(0)
+            relay_weights(0)
+            begin(heavy[2][3], heavy[2][4])
+        if k == 1:
+            forward_x(1)
+            pass_near.wait_recv()
+        if k == 2:
+            onwards[0].wait_recv()
+        if k == 3:
+            onwards[1].wait_recv()
+
+    def project_step(k, carry):
+        for i in range(4):
+            pl.when(k == i)(functools.partial(arrive, i))
+        unit = jnp.where(k < 2, 2 * mine + lax.rem(lax.rem(z, 2) + k, 2), 2 * other + k - 2)
+        project(unit)
+        return carry
+
+    lax.fori_loop(0, 4, project_step, 0)
+    saves = [
+        pltpu.make_async_copy(src, dst, local.at[6 + i])
+        for i, (src, dst) in enumerate(
+            ((segk, segk_o), (qn, qn_o), (kn, kn_o), (vn, vn_o), (qt, qt_o), (kt, kt_o), (xst, xst_o), (wgf, wgf_o))
+        )
+    ]
+    for save in saves:
+        save.start()
+
     homes = []
     for u in range(4):
         unit = unit_place(me, u)
@@ -828,21 +835,21 @@
                 move.start()
 
     def between(i):
-        if i == 0:
-            relay_weights(0)
+        if i == 2:
+            relay_weights(1)
         if i == per_unit:
             send_home(0)
-            relay_weights(1)
+        if i == per_unit + 1:
+            relay_diag(0)
         if i == 2 * per_unit:
             send_home(1)
-            relay_diag(0)
         if i == 3 * per_unit:
             send_home(2)
+        if i == 3 * per_unit + 1:
             relay_weights(2)
-            relay_diag(1)
 
     def tile_step(i, carry):
-        for point in range(0, steps, per_unit):
+        for point in (2, per_unit, per_unit + 1, 2 * per_unit, 3 * per_unit, 3 * per_unit + 1):
             pl.when(i == point)(functools.partial(between, point))
         tile = unit_place(me, i // per_unit) * per_unit + lax.rem(i, per_unit)
         forward_tile(tile, rand, segq, segk, qt, kn, vt, q3, tbuf, att, otile, lse)
@@ -857,12 +864,13 @@
     for save in last:
         save.start()
     home[t] = att[rows_of(t), :]
-    relay_diag(2)
     for u, move in homes:
         move.wait()
     for s in range(2):
         pieces = [home[4 * s + g].astype(F32) for g in range(4)]
         att_out[tok * s : tok * (s + 1), :] = jnp.concatenate(pieces, axis=1).astype(BF16)
+    relay_diag(1)
+    relay_diag(2)
     for to_x, to_y, dy, px, dx, py, pd in tail:
         px.wait_recv()
         py.wait_recv()
@@ -1068,7 +1076,9 @@
             own[yy, xx, zz] = plus(own[yy, xx, zz], ra[yy, xx, zz]).astype(BF16)
 
         each(16, fold)
-        begin(bx, by)
+
+    def cross(work):
+        begin(work[1][2], work[1][3])
 
     def stage_b(work):
         (o, own, ra, rb1, rb2, rc, rd), (swap_core, load, bx, by, cy, cx, ds) = work
@@ -1118,23 +1128,43 @@
     per_unit = 2 * tok // TILE
     steps = dqkv.shape[0] // TILE
 
-    def before_unit(u):
+    def unit_arrives(u):
         for v, move in dat_moves:
             if u == v:
                 move.wait_recv()
-        if u == 1:
-            for work in works:
-                stage_a(work)
-            stat_step(1)
-        if u == 2:
-            stat_step(2)
-        if u == 3:
-            stage_b(works[0])
-            stat_step(3)
+
+    def step_one():
+        stage_a(works[0])
+        cross(works[0])
+
+    def step_two():
+        stage_a(works[1])
+        stat_step(1)
+
+    def step_seven():
+        stage_b(works[0])
+        cross(works[1])
+        cross(works[2])
+
+    events = {
+        1: [step_one],
+        2: [step_two],
+        4: [functools.partial(stage_a, works[2]), functools.partial(stat_step, 2)],
+        7: [step_seven],
+        8: [functools.partial(stat_step, 3)],
+        10: [functools.partial(stage_c, works[0])],
+    }
+    for u in range(4):
+        events.setdefault(u * per_unit, []).append(functools.partial(unit_arrives, u))
 
     def tile_step(i, carry):
-        for u in range(4):
-            pl.when(i == u * per_unit)(functools.partial(before_unit, u))
+        for point, actions in sorted(events.items()):
+
+            @pl.when(i == point)
+            def _():
+                for action in actions:
+                    action()
+
         tile = unit_place(me, 3 - i // per_unit) * per_unit + lax.rem(i, per_unit)
         backward_tile(
             tile, dat, qn, qt, otile, lse, rand, segq, segk, kn, vn, kt, dqkv,
@@ -1143,8 +1173,6 @@
         return carry
 
     lax.fori_loop(0, steps, tile_step, 0)
-    stage_b(works[1])
-    stage_b(works[2])
     stat_step(4)
     loads[9].wait()
 
@@ -1160,7 +1188,8 @@
         core = cps.to(part.at[zz, 1 - c], rp.at[zz], me.partner)
         begin(core)
         cores.append(core)
-    stage_c(works[0])
+    stage_b(works[1])
+    stage_b(works[2])
 
     up = [cps.to(own_p.at[2 * other + j], rb_p.at[j], me.at_z(me.pair_z)) for j in range(2)]
     near = cps.to(own_p.at[me.pair_z], ra_p, me.at_z(me.pair_z))

time: 262 us -> 221 us (0.84)
  Pallas kernels: 211 us -> 170 us
    pallas_call x1, Pallas kernels: 91.8 us -> 68.4 us  [forward_half(): pl.pallas_call(forward_kernel, in_specs=[VMEMSPACE] * 2 + [ANYSPACE] * 3...]
    pallas_call x1, Pallas kernels: 119 us -> 102 us  [backward_half(): pl.pallas_call(backward_kernel, in_specs=[VMEMSPACE] * 2 + [ANYSPACE] * 3...]
where the time goes in v1:
time: 221 us
  Pallas kernels  170 us (77%)
  matrix products  25 us (11%)
  local copies, waits for them, and re-layouts  17.4 us (8%)
  other arithmetic  7.36 us (3%)
    pallas_call x1, Pallas kernels, backward_half(): pl.pallas_call(backward_kernel, in_specs=[VMEMSPACE] * 2 + [ANYSPACE] * 3...  102 us
    pallas_call x1, Pallas kernels, forward_half(): pl.pallas_call(forward_kernel, in_specs=[VMEMSPACE] * 2 + [ANYSPACE] * 3...  68.4 us
    dot_general x3, matrix products, product_tn(): lax.dot_general(left_side, right_side, (((0,), (0,)), ((), ())), preferre...  10.9 us
    dot_general x3, matrix products, product_nt(): lax.dot_general(left_side, right_side, (((1,), (1,)), ((), ())), preferre...  7.25 us
    dot_general x3, matrix products, product(): return jnp.dot(left_side, right_side, preferred_element_type=jnp.float32)  6.91 us
    unnamed x43, local copies, waits for them, and re-layouts  5.95 us

profile of v1, /device:TPU:0, one launch (start us, length us, event | category | flops | bytes accessed | tf_op | source)
XLA Modules:
  0.0 220.9 jit_solution(4956159429817497504)
XLA Ops:
  0.6 0.0 copy-start
  0.7 0.7 copy-done
  1.4 1.3 dynamic-slice_bitcast_fusion.refs_6_
  2.7 0.8 slice_reduce_fusion
  3.5 1.4 convert_reduce_fusion
  5.0 0.1 div.42
  5.1 0.1 copy.26
  5.1 0.4 copy.27
  5.5 0.2 broadcast_in_dim.2
  5.7 0.8 reshape.131.refs_5_
  6.5 1.1 reshape.128
  7.6 0.6 constant_dynamic-slice_fusion.2
  8.3 0.3 copy.30
  8.5 0.2 pad.4.clone
  8.7 0.8 copy.31
  9.5 68.4 %forward_half.1 = (bf16[4,192,768]{2,1,0:T(8,128)(2,1)}, bf16[4,192,3072]{2,1,0:T(8,128)(2,1)}, bf16[4,768,768]{2,1,0:T(8,128)(2,1)}, bf16[384,768]{1,0:T(8,128)...) custom-call(bf16[2,192,768]{2,1,0:T(8,128)(2,1)} %refs_0_.1, ...), custom_call_target="tpu_custom_call" | custom-call | tf_op jit(solution)/shard_map/forward_half/pallas_call | solution.py:900
  77.9 2.3 %fusion.22 = (f32[384]{0:T(512)S(1)}, f32[384,768]{1,0:T(8,128)S(1)}) fusion(bf16[384,768]{1,0:T(8,128)(2,1)} %get-tuple-element.28, bf16[768,768]{1,0:T(8,128)(2,1)} %bitcast.53, bf16[384,768]{1,0:T(8,128)(2,1)S(1)} %bitcast.59), kind=kOutput, calls=%fused_computation.63 | convolution fusion | flops 453869184 | bytes 3540480 | tf_op jit(solution)/shard_map/dot_general | solution.py:56
  80.2 0.3 multiply_reduce_fusion.3
  80.5 0.3 copy-done.12
  80.8 2.4 %multiply_convert_fusion = (bf16[384,3072]{1,0:T(8,128)(2,1)S(1)}, f32[384,3072]{1,0:T(8,128)S(1)}) fusion(bf16[768,3072]{1,0:T(8,128)(2,1)S(1)} %bitcast.65, f32[384,768]{1,0:T(8,128)S(1)} %get-tuple-element.65, f32[768]{0:T(1024)S(1)} %get-tuple-element.59, f32[768]{0:T(1024)S(1)} %get-tuple-element.71, f32[384]{0:T(512)S(1)} %add_rsqrt_fusion.1, ...), kind=kOutput, calls=%fused_computation.9 | convolution fusion | flops 1819312128 | bytes 12985344 | tf_op jit(solution)/shard_map/dot_general | solution.py:56
  83.3 2.1 fusion.23
  85.4 0.3 multiply_reduce_fusion.2
  85.7 0.8 copy-done.1
  86.5 0.6 fusion.12
  87.1 1.3 fusion.9
  88.4 3.4 %fusion.5 = bf16[384,3072]{1,0:T(8,128)(2,1)S(1)} fusion(f32[384,3072]{1,0:T(8,128)S(1)} %get-tuple-element.67, bf16[3072,768]{1,0:T(8,128)(2,1)S(1)} %bitcast.70, f32[384,768]{1,0:T(8,128)S(1)} %get-tuple-element.60), kind=kOutput, calls=%fused_computation.8 | convolution fusion | flops 1824030720 | bytes 12976128 | tf_op jit(solution)/shard_map/dot_general | solution.py:66
  91.8 2.4 %multiply_reduce_fusion = (f32[768]{0:T(1024)S(1)}, f32[384]{0:T(512)S(1)}, f32[384]{0:T(512)S(1)}, f32[768]{0:T(1024)S(1)}, f32[384,768]{1,0:T(8,128)S(1)}) fusion(f32[384,768]{1,0:T(8,128)S(1)} %get-tuple-element.65, f32[384]{0:T(512)S(1)} %add_rsqrt_fusion.1, f32[384]{0:T(512)S(1)} %broadcast_multiply_fusion.5, f32[768]{0:T(1024)S(1)} %get-tuple-element.71, ...), kind=kOutput, calls=%fused_computation.27 | convolution fusion | flops 1814886144 | bytes 10632192 | tf_op jit(solution)/shard_map/dot_general | solution.py:66
  94.2 0.4 subtract_multiply_fusion
  94.6 0.9 copy-done.2
  95.5 1.5 convolution_convert_fusion.3
  97.0 0.6 pad_maximum_fusion.refs_1_
  97.6 2.3 %reshape.137 = bf16[2,192,4,192]{3,2,1,0:T(4,128)(2,1)S(1)} reshape(bf16[384,768]{1,0:T(8,128)(2,1)} %convolution_convert_fusion.3) | data formatting | bytes 1179648 | tf_op jit(solution)/shard_map/reshape | solution.py:1397
  99.9 1.0 copy.28
  100.8 0.2 copy-done.4
  101.0 1.8 convolution_convert_fusion.2
  102.9 4.7 %convolution_convert_fusion.1 = bf16[768,3072]{1,0:T(8,128)(2,1)} fusion(bf16[384,3072]{1,0:T(8,128)(2,1)S(1)} %copy-done.16, f32[384,768]{1,0:T(8,128)S(1)} %get-tuple-element.65, f32[768]{0:T(1024)S(1)} %get-tuple-element.59, f32[768]{0:T(1024)S(1)} %get-tuple-element.71, f32[384]{0:T(512)S(1)} %add_rsqrt_fusion.1, f32[384]{0:T(512)S(1)} %broadcast_multiply_fusion.5), kind=kOutput, calls=%fused_computation.2 | convolution fusion | flops 1815773184 | bytes 8266752 | tf_op jit(solution)/shard_map/dot_general | solution.py:60
  107.6 4.3 %convolution_convert_fusion = bf16[3072,768]{1,0:T(8,128)(2,1)} fusion(bf16[384,3072]{1,0:T(8,128)(2,1)S(1)} %copy-done.14, f32[384,768]{1,0:T(8,128)S(1)} %copy-done.6), kind=kOutput, calls=%fused_computation.1 | convolution fusion | flops 1814593536 | bytes 8257536 | tf_op jit(solution)/shard_map/dot_general | solution.py:60
  111.9 101.7 %backward_half.1 = (f32[24,768]{1,0:T(8,128)}, f32[24,3072]{1,0:T(8,128)}, f32[96,768]{1,0:T(8,128)}, f32[4,768]{1,0:T(4,128)}, f32[2,192,768]{2,1,0:T(8,128)}, /*index=5*/f32[4,24,768]{2,1,0:T(8,128)}) custom-call(bf16[8,192,192]{2,1,0:T(8,128)(2,1)} %bitcast.58, f32[4,768]{1,0:T(4,128)} %pad_maximum_fusion.refs_1_, ...), custom_call_target="tpu_custom_call" | custom-call | tf_op jit(solution)/shard_map/backward_half/pallas_call | solution.py:1303
  213.6 2.6 %add.97 = f32[2,192,768]{2,1,0:T(8,128)} add(f32[2,192,768]{2,1,0:T(8,128)} %get-tuple-element.42, f32[2,192,768]{2,1,0:T(8,128)S(1)} %bitcast.52) | non-fusion elementwise | flops 294912 | bytes 3538944 | tf_op jit(solution)/shard_map/add | solution.py:1410
  216.1 0.8 constant_dynamic-slice_fusion
  216.9 0.6 fusion.21
  217.5 0.2 reshape.143
  217.7 0.1 slice_bitcast_fusion
  217.7 0.2 copy.29
  217.9 0.9 reshape.144
  218.8 0.6 copy.37
  219.4 0.7 copy.38
  220.2 0.7 copy.39
  (47 shorter events, 0.2 us)
Async XLA Ops:
  0.6 0.8 copy-start
  0.6 5.9 %copy-start.7 = (bf16[192,2304]{1,0:T(8,128)(2,1)S(1)}, bf16[192,2304]{1,0:T(8,128)(2,1)}, u32[]{:S(2)}) copy-start(bf16[192,2304]{1,0:T(8,128)(2,1)} %param.13) | copy-start | bytes 2654212
  9.5 68.4 %copy-start.3 = (bf16[2,192,768]{2,1,0:T(8,128)(2,1)S(1)}, bf16[2,192,768]{2,1,0:T(8,128)(2,1)}, u32[]{:S(2)}) copy-start(bf16[2,192,768]{2,1,0:T(8,128)(2,1)} %refs_0_.1) | copy-start | bytes 1769476
  77.9 2.9 %copy-start.12 = (bf16[4,192,3072]{2,1,0:T(8,128)(2,1)S(1)}, bf16[4,192,3072]{2,1,0:T(8,128)(2,1)}, u32[]{:S(2)}) copy-start(bf16[4,192,3072]{2,1,0:T(8,128)(2,1)} %get-tuple-element.30) | copy-start | bytes 14155780
  80.2 3.0 %slice-start = ((s8[4718592]{0:T(1024)(128)(4,1)}), s8[4194304]{0:T(1024)(128)(4,1)S(1)}, s32[]{:S(2)}) async-start(s8[4718592]{0:T(1024)(128)(4,1)} %bitcast.67), calls=%async_computation | async-start | bytes 8388608
  80.8 2.5 %slice-start.1 = ((s8[4718592]{0:T(1024)(128)(4,1)}), s8[524288]{0:T(1024)(128)(4,1)S(1)}, s32[]{:S(2)}) async-start(s8[4718592]{0:T(1024)(128)(4,1)} %bitcast.67), calls=%async_computation.1 | async-start | bytes 1048576
  83.2 2.2 copy-start.13
  85.4 1.1 copy-start.1
  88.4 3.4 %copy-start.5 = (f32[384,768]{1,0:T(8,128)}, f32[384,768]{1,0:T(8,128)S(1)}, u32[]{:S(2)}) copy-start(f32[384,768]{1,0:T(8,128)S(1)} %get-tuple-element.60) | copy-start | bytes 3538948
  91.8 2.4 %copy-start.15 = (bf16[384,3072]{1,0:T(8,128)(2,1)}, bf16[384,3072]{1,0:T(8,128)(2,1)S(1)}, u32[]{:S(2)}) copy-start(bf16[384,3072]{1,0:T(8,128)(2,1)S(1)} %fusion.5) | copy-start | bytes 7077892
  94.2 1.3 copy-start.2
  99.8 1.2 copy-start.4
  101.0 1.8 copy-start.16
  102.9 4.7 %copy-start.6 = (f32[384,768]{1,0:T(8,128)S(1)}, f32[384,768]{1,0:T(8,128)}, u32[]{:S(2)}) copy-start(f32[384,768]{1,0:T(8,128)} %copy-done.5) | copy-start | bytes 3538948
  102.9 4.7 %copy-start.14 = (bf16[384,3072]{1,0:T(8,128)(2,1)S(1)}, bf16[384,3072]{1,0:T(8,128)(2,1)}, u32[]{:S(2)}) copy-start(bf16[384,3072]{1,0:T(8,128)(2,1)} %copy-done.13) | copy-start | bytes 7077892
  213.6 3.9 %copy-start.10 = (f32[4,24,768]{2,1,0:T(8,128)S(1)}, f32[4,24,768]{2,1,0:T(8,128)}, u32[]{:S(2)}) copy-start(f32[4,24,768]{2,1,0:T(8,128)} %get-tuple-element.43) | copy-start | bytes 884740
  217.5 1.3 copy-start.11
  217.6 1.8 copy-start.9
  217.6 2.5 %copy-start.8 = (f32[96,768]{1,0:T(8,128)S(1)}, f32[96,768]{1,0:T(8,128)}, u32[]{:S(2)}) copy-start(f32[96,768]{1,0:T(8,128)} %get-tuple-element.86) | copy-start | bytes 884740

commit v2 on v1

--- a/solution.py
+++ b/solution.py
@@ -568,11 +568,19 @@
         return (self.d, 2 * z + self.c)
 
 
-def meet(devices):
+def greet(devices):
     barrier = pltpu.get_barrier_semaphore()
     for device in devices:
         pl.semaphore_signal(barrier, inc=1, device_id=device, device_id_type=MESH)
-    pl.semaphore_wait(barrier, len(devices))
+
+
+def met(devices):
+    pl.semaphore_wait(pltpu.get_barrier_semaphore(), len(devices))
+
+
+def meet(devices):
+    greet(devices)
+    met(devices)
 
 
 def tile_tables(tile, rand_ref, segq_ref, blocks):
@@ -991,13 +999,17 @@
 
 
 def backward_kernel(*refs):
-    (src, stats, g0, g1, g2), refs = refs[:5], refs[5:]
+    (da, stats, g2), refs = refs[:3], refs[3:]
     (rand, segq), refs = refs[:2], refs[2:]
+    extra, refs = refs[:5], refs[5:]
     saved, refs = refs[:10], refs[10:]
     (o0, o1, o2, stats_out, ig, wq), refs = refs[:6], refs[6:]
     bufs, refs = refs[:18], refs[18:]
     held, refs = refs[:10], refs[10:]
     kn, vn, kt, segk, qn, qt, otile, lse, xst, wg = held
+    more, refs = refs[:5], refs[5:]
+    wo, hb, dpre, at, resid = more
+    (src, rows_t), refs = refs[:2], refs[2:]
     (dat, dqkv, q3t, d3t, q3, d3, dk, dv), refs = refs[:8], refs[8:]
     (part, own_p, rp, ra_p, rb_p, ro, dwg, wb1, wb2, wc, wr), refs = refs[:11], refs[11:]
     nsend, nrecv, send, recv, local = refs
@@ -1012,9 +1024,20 @@
         pltpu.make_async_copy(from_hbm, to_vmem, local.at[4 + i])
         for i, (from_hbm, to_vmem) in enumerate(zip(saved, held))
     ]
-    for load in loads:
+    more_loads = [
+        pltpu.make_async_copy(from_hbm, to_vmem, local.at[14 + i])
+        for i, (from_hbm, to_vmem) in enumerate(zip(extra, more))
+    ]
+    friends = [me.across_x, me.across_y] + [(me.d, lax.rem(t + k, 8)) for k in range(1, 8)]
+    greet(friends)
+    for load in more_loads[:4] + loads + more_loads[4:]:
         load.start()
-    meet([me.across_x, me.across_y] + [(me.d, lax.rem(t + k, 8)) for k in range(1, 8)])
+    more_loads[0].wait()
+    for g in range(4):
+        both = nt(da[...], wo[g]).astype(BF16)
+        src[g] = both[:tok]
+        src[4 + g] = both[tok:]
+    met(friends)
     cps = Copies(send, recv)
 
     def rows_of(index):
@@ -1032,12 +1055,14 @@
     keep.start()
 
     works = []
-    for i, (g, o) in enumerate(((g2, o2), (g1, o1), (g0, o0))):
+    for i, o in enumerate((o2, o1, o0)):
         own, ra, rb1, rb2, rc, rd = bufs[6 * i : 6 * i + 6]
-        swap_core = cps.to(g.at[:, :, :, 1 - c], ra, me.partner)
-        swap_core.start()
-        load = pltpu.make_async_copy(g.at[:, :, :, c], own, local.at[i])
-        load.start()
+        if i == 0:
+            away = g2.at[:, :, :, 1 - c]
+            load = pltpu.make_async_copy(g2.at[:, :, :, c], own, local.at[0])
+        else:
+            away, own, load = own.at[:, :, :, 1 - c], own.at[:, :, :, c], None
+        swap_core = cps.to(away, ra, me.partner)
         moves = (
             swap_core,
             load,
@@ -1068,7 +1093,8 @@
 
     def stage_a(work):
         (o, own, ra, rb1, rb2, rc, rd), (swap_core, load, bx, by, cy, cx, ds) = work
-        load.wait()
+        if load is not None:
+            load.wait()
         swap_core.wait_recv()
 
         def fold(i):
@@ -1114,6 +1140,32 @@
             cp.wait_recv()
         o[...] = plus(rc[z], rd[0]) + plus(rd[1], rd[2])
 
+    stat_step(0)
+    down_work, up_work, out_work = works
+    down_work[1][0].start()
+    down_work[1][1].start()
+
+    def weight_grad(tokens, cotangent, total):
+        rows_t[...] = tokens[...].astype(F32).T.astype(BF16)
+        size, wide = rows_t.shape[0] // 4, 768
+        count = cotangent.shape[1] // wide
+
+        def block(i):
+            r, k = i // count, lax.rem(i, count)
+            cols = pl.ds(pl.multiple_of(k * wide, wide), wide)
+            grad = nn(rows_t[pl.ds(pl.multiple_of(r * size, size), size), :], cotangent[:, cols])
+            total[r // 2, lax.rem(r, 2), :, :, :, cols] = grad.astype(BF16).reshape(
+                total.shape[2:5] + (wide,)
+            )
+
+        each(4 * count, block)
+
+    for load in more_loads[1:4]:
+        load.wait()
+    weight_grad(at, da, bufs[12])
+    out_work[1][0].start()
+    weight_grad(hb, dpre, bufs[6])
+    up_work[1][0].start()
     q3t[...] = jnp.zeros_like(q3t)
     d3t[...] = jnp.zeros_like(d3t)
     dk[...] = jnp.zeros_like(dk)
@@ -1121,7 +1173,6 @@
     gap = jnp.zeros((dqkv.shape[0], 256 - NH * HEAD), BF16)
     for g in range(3):
         dqkv[:, 256 * g + NH * HEAD : 256 * (g + 1)] = gap
-    stat_step(0)
     for load in loads[:8]:
         load.wait()
     keep.wait()
@@ -1134,25 +1185,21 @@
                 move.wait_recv()
 
     def step_one():
-        stage_a(works[0])
-        cross(works[0])
+        stat_step(1)
+        stage_a(out_work)
+        cross(out_work)
 
     def step_two():
-        stage_a(works[1])
-        stat_step(1)
-
-    def step_seven():
-        stage_b(works[0])
-        cross(works[1])
-        cross(works[2])
+        stat_step(2)
+        stage_a(down_work)
+        cross(down_work)
 
     events = {
         1: [step_one],
         2: [step_two],
-        4: [functools.partial(stage_a, works[2]), functools.partial(stat_step, 2)],
-        7: [step_seven],
-        8: [functools.partial(stat_step, 3)],
-        10: [functools.partial(stage_c, works[0])],
+        5: [functools.partial(stage_a, up_work)],
+        7: [functools.partial(stage_b, out_work)],
+        10: [functools.partial(stat_step, 3)],
     }
     for u in range(4):
         events.setdefault(u * per_unit, []).append(functools.partial(unit_arrives, u))
@@ -1180,7 +1227,9 @@
     dqkv[:, 512 : 512 + NH * HEAD] = dv[...].astype(BF16)
     order = [2 * other, 2 * other + 1, me.pair_z, z]
     cores = []
-    for zz in order:
+
+    def partial_grad(k):
+        zz = order[k]
         rows = pl.ds(pl.multiple_of(zz * 2 * tok, 2 * tok), 2 * tok)
         grad = nt(dqkv[rows, :], wg[...]).astype(BF16)
         part[zz, 0] = grad[:tok]
@@ -1188,18 +1237,38 @@
         core = cps.to(part.at[zz, 1 - c], rp.at[zz], me.partner)
         begin(core)
         cores.append(core)
-    stage_b(works[1])
-    stage_b(works[2])
+
+    def merge_cores(k):
+        zz = order[k]
+        cores[k].wait_recv()
+        own_p[zz] = plus(part[zz, c], rp[zz]).astype(BF16)
 
     up = [cps.to(own_p.at[2 * other + j], rb_p.at[j], me.at_z(me.pair_z)) for j in range(2)]
     near = cps.to(own_p.at[me.pair_z], ra_p, me.at_z(me.pair_z))
-    for k, zz in enumerate(order):
-        cores[k].wait_recv()
-        own_p[zz] = plus(part[zz, c], rp[zz]).astype(BF16)
-        if k < 2:
-            pl.when(is_outer)(up[k].start)
-        if k == 2:
-            begin(near)
+    down_send, down_recv = cps.used, cps.used
+    cps.used += 2
+    down = [
+        pltpu.make_async_remote_copy(
+            src_ref=own_p.at[2 * other + j], dst_ref=ro, send_sem=send.at[down_send + j],
+            recv_sem=recv.at[down_recv], device_id=me.at_z(2 * other + j), device_id_type=MESH,
+        )
+        for j in range(2)
+    ]
+
+    partial_grad(0)
+    partial_grad(1)
+    merge_cores(0)
+    pl.when(is_outer)(up[0].start)
+    partial_grad(2)
+    merge_cores(1)
+    pl.when(is_outer)(up[1].start)
+    partial_grad(3)
+    stage_b(down_work)
+    cross(up_work)
+    merge_cores(2)
+    begin(near)
+    merge_cores(3)
+    stage_c(out_work)
     loads[8].wait()
     half_rows = xst.shape[0] // 2
     for yy in range(2):
@@ -1208,15 +1277,6 @@
     bx = cps.to(dwg.at[:, 1 - x, 0:4], wb1, me.across_x)
     by = cps.to(dwg.at[1 - y, :, 4:8], wb2, me.across_y)
     begin(bx, by)
-    down_send, down_recv = cps.used, cps.used
-    cps.used += 2
-    down = [
-        pltpu.make_async_remote_copy(
-            src_ref=own_p.at[2 * other + j], dst_ref=ro, send_sem=send.at[down_send + j],
-            recv_sem=recv.at[down_recv], device_id=me.at_z(2 * other + j), device_id_type=MESH,
-        )
-        for j in range(2)
-    ]
 
     @pl.when(is_middle)
     def _():
@@ -1225,8 +1285,8 @@
             own_p[2 * other + j] = plus(own_p[2 * other + j], rb_p[j]).astype(BF16)
             down[j].start()
 
-    stage_c(works[1])
-    stage_c(works[2])
+    stage_c(down_work)
+    stage_b(up_work)
     bx.wait_recv()
 
     def fold_x(i):
@@ -1245,8 +1305,7 @@
     each(8, fold_y)
     cx = cps.to(wb2.at[1 - x], wc.at[4:8], me.across_x)
     begin(cx)
-    stat_all[-1].wait_recv()
-    stats_out[...] = nsend[4] + nrecv[4]
+    stage_c(up_work)
     cy.wait_recv()
     cx.wait_recv()
 
@@ -1260,17 +1319,21 @@
         peer = lax.rem(t + k, 8)
         moves.append(cps.to(wc.at[peer], wr.at[t], (me.d, peer)))
     begin(*moves)
+    stat_all[-1].wait_recv()
+    stats_out[...] = nsend[4] + nrecv[4]
     near.wait_recv()
-    ig[mine] = plus(own_p[z], ra_p[...])
+    more_loads[4].wait()
+    ig[mine] = resid[mine] + plus(own_p[z], ra_p[...])
     down[0].wait_recv()
-    ig[other] = ro[...].astype(F32)
-    for work in works:
-        stage_d(work)
+    ig[other] = resid[other] + ro[...].astype(F32)
+    stage_d(out_work)
+    stage_d(down_work)
     wr[t] = wc[t]
     for move in moves:
         move.wait_recv()
     for g in range(4):
         wq[g] = plus(wr[g], wr[4 + g])
+    stage_d(up_work)
     for cp in sent + stat_all + [move for u, move in dat_moves] + [moves[0] for refs, moves in works]:
         cp.wait_send()
 
@@ -1285,14 +1348,15 @@
             cp.wait_send()
 
 
-def backward_half(src, stats, grads, rand, segq, saved):
-    dims = [g.shape[-2:] for g in grads]
-    tok = src.shape[1]
+def backward_half(da, stats, down_grad, rand, segq, extra, saved):
     features, length = saved[8].shape
+    wide = extra[2].shape[1]
+    dims = [(features // 32, features), (features // 32, wide), (wide // 32, features)]
+    tok = da.shape[0] // 2
     bufs = []
-    for rows, cols in dims[::-1]:
+    for i, (rows, cols) in enumerate(dims[::-1]):
         bufs += [
-            pltpu.VMEM((2, 2, 4, rows, cols), BF16),
+            pltpu.VMEM(((2, 2, 4, 2) if i else (2, 2, 4)) + (rows, cols), BF16),
             pltpu.VMEM((2, 2, 4, rows, cols), BF16),
             pltpu.VMEM((2, 2, rows, cols), BF16),
             pltpu.VMEM((2, 2, rows, cols), BF16),
@@ -1302,7 +1366,7 @@
     wrows = features // 32
     return pl.pallas_call(
         backward_kernel,
-        in_specs=[VMEMSPACE] * 2 + [ANYSPACE] * 3 + [VMEMSPACE] * 2 + [ANYSPACE] * 10,
+        in_specs=[VMEMSPACE] * 2 + [ANYSPACE] + [VMEMSPACE] * 2 + [ANYSPACE] * 15,
         out_specs=[VMEMSPACE] * 6,
         out_shape=[jax.ShapeDtypeStruct(dim, F32) for dim in dims]
         + [
@@ -1311,8 +1375,10 @@
             jax.ShapeDtypeStruct((4, wrows, 768), F32),
         ],
         scratch_shapes=bufs
-        + [pltpu.VMEM(a.shape, a.dtype) for a in saved]
+        + [pltpu.VMEM(a.shape, a.dtype) for a in saved + extra]
         + [
+            pltpu.VMEM((8, tok, NH * HEAD), BF16),
+            pltpu.VMEM((features, 2 * tok), BF16),
             pltpu.VMEM((length, NH * HEAD), BF16),
             pltpu.VMEM((length, 768), BF16),
             pltpu.VMEM((256, NH * TILE), BF16),
@@ -1336,13 +1402,13 @@
             pltpu.VMEM((5,) + stats.shape, F32),
             pltpu.SemaphoreType.DMA((90,)),
             pltpu.SemaphoreType.DMA((90,)),
-            pltpu.SemaphoreType.DMA((14,)),
+            pltpu.SemaphoreType.DMA((19,)),
         ],
         compiler_params=pltpu.CompilerParams(
             collective_id=3, has_side_effects=True, vmem_limit_bytes=62 * 1024 * 1024
         ),
         name="backward_half",
-    )(src, stats, *grads, rand, segq, *saved)
+    )(da, stats, down_grad, rand, segq, *extra, *saved)
 
 
 def head_layout(
@@ -1386,20 +1452,16 @@
     grad_branch = grad_resid_two.astype(BF16)
     grad_down_w = product_tn(activated, grad_branch).astype(BF16)
     grad_pre = (product_nt(grad_branch, full_down) * gelu_slope(pre_act)).astype(BF16)
-    grad_up_w = product_tn(hidden_low, grad_pre).astype(BF16)
     grad_hidden = grad_resid_two + product_nt(grad_pre, full_up)
     grad_resid_one, gain_one, shift_one = norm_backward(
         grad_hidden, normed_one, inv_one, norm_gain[0]
     )
     grad_mix = grad_resid_one.astype(BF16)
-    grad_out_w = product_tn(att_flat, grad_mix).astype(BF16)
-    grad_att = product_nt(grad_mix, full_out).astype(BF16)
-    grad_att = grad_att.reshape(seqs, tok, groups, width).transpose(0, 2, 1, 3)
-    src = grad_att.reshape(seq, tok, width)
     stats = jnp.stack([gain_one, gain_two, shift_one, shift_two])
-    cut = lambda g: g.reshape(2, 2, 4, 2, g.shape[0] // 32, g.shape[1])
+    grad_down_w = grad_down_w.reshape(2, 2, 4, 2, grad_down_w.shape[0] // 32, features)
     out_sum, up_sum, down_sum, stats, ig, wq = backward_half(
-        src, stats, [cut(grad_out_w), cut(grad_up_w), cut(grad_down_w)], rand, segq,
+        grad_mix, stats, grad_down_w, rand, segq,
+        (wof, hidden_low, grad_pre, att_flat, grad_resid_one.reshape(seqs, tok, features)),
         (kn, vn, kt, segk, qn, qt, otile, lse, xst, wgf),
     )
     wq = wq.reshape(groups, features // 32, 3, 256)[..., :width].transpose(1, 2, 0, 3)
@@ -1407,7 +1469,7 @@
     stats = lax.dynamic_slice_in_dim(stats, mine * (features // 32), features // 32, 1)
     return (
         result.astype(BF16).reshape(seqs, tok, features),
-        ig + grad_resid_one.reshape(seqs, tok, features),
+        ig,
         wq.reshape(features // 32, 3 * features),
         out_sum,
         up_sum,

time: 221 us -> 212 us (0.959)
  matrix products: 25 us -> 17.2 us
  local copies, waits for them, and re-layouts: 17.4 us -> 14.9 us
    dot_general x3 -> x1, matrix products: 10.9 us -> 4.29 us  [product_tn(): lax.dot_general(left_side, right_side, (((0,), (0,)), ((), ())), preferre...]
    reshape x2 -> x0, local copies, waits for them, and re-layouts: 3.25 us -> none  [head_layout(): grad_att = grad_att.reshape(seqs, tok, groups, width).transpose(0, 2, 1, 3)]
    add x1 -> x0, other arithmetic: 2.56 us -> none  [head_layout(): ig + grad_resid_one.reshape(seqs, tok, features)]
    dot_general x3 -> x2, matrix products: 7.25 us -> 5.65 us  [product_nt(): lax.dot_general(left_side, right_side, (((1,), (1,)), ((), ())), preferre...]
    unnamed x43 -> x32, local copies, waits for them, and re-layouts: 5.95 us -> 5.63 us
where the time goes in v2:
time: 212 us; the launch traced here: 211 us
  Pallas kernels  172 us (81%)
  matrix products  17.2 us (8%)
  local copies, waits for them, and re-layouts  14.9 us (7%)
  other arithmetic  6.39 us (3%)
    pallas_call x1, Pallas kernels, backward_half(): pl.pallas_call(backward_kernel, in_specs=[VMEMSPACE] * 2 + [ANYSPACE] + [...  104 us
    pallas_call x1, Pallas kernels, forward_half(): pl.pallas_call(forward_kernel, in_specs=[VMEMSPACE] * 2 + [ANYSPACE] * 3...  68.4 us
    dot_general x3, matrix products, product(): return jnp.dot(left_side, right_side, preferred_element_type=jnp.float32)  7.28 us
    dot_general x2, matrix products, product_nt(): lax.dot_general(left_side, right_side, (((1,), (1,)), ((), ())), preferre...  5.65 us
    unnamed x32, local copies, waits for them, and re-layouts  5.63 us
    dot_general x1, matrix products, product_tn(): lax.dot_general(left_side, right_side, (((0,), (0,)), ((), ())), preferre...  4.29 us

profile of v2, /device:TPU:0, one launch (start us, length us, event | category | flops | bytes accessed | tf_op | source)
XLA Modules:
  0.0 211.4 jit_solution(11261962739787347089)
XLA Ops:
  0.6 0.0 copy-start
  0.6 0.0 copy-start.6
  0.7 0.7 copy-done
  1.4 1.3 dynamic-slice_bitcast_fusion.refs_6_.refs_4_
  2.7 0.8 slice_reduce_fusion
  3.5 1.4 convert_reduce_fusion
  5.0 0.1 div.42
  5.0 0.1 copy.24
  5.1 0.4 copy.25
  5.5 0.2 broadcast_in_dim.2
  5.7 0.8 reshape.119.refs_5_.refs_3_
  6.5 0.0 copy-done.6
  6.5 1.1 reshape.116
  7.6 0.6 constant_dynamic-slice_fusion.2
  8.3 0.3 copy.27
  8.5 0.2 pad.4.clone
  8.7 0.8 copy.28
  9.5 68.4 %forward_half.1 = (bf16[4,192,768]{2,1,0:T(8,128)(2,1)}, bf16[4,192,3072]{2,1,0:T(8,128)(2,1)}, bf16[4,768,768]{2,1,0:T(8,128)(2,1)}, bf16[384,768]{1,0:T(8,128)...) custom-call(bf16[2,192,768]{2,1,0:T(8,128)(2,1)} %refs_0_.1, ...), custom_call_target="tpu_custom_call" | custom-call | tf_op jit(solution)/shard_map/forward_half/pallas_call | solution.py:908
  77.9 0.0 copy-done.3
  77.9 2.3 %fusion.18 = (f32[384]{0:T(512)S(1)}, f32[384,768]{1,0:T(8,128)S(1)}) fusion(bf16[384,768]{1,0:T(8,128)(2,1)} %get-tuple-element.28.refs_8_, bf16[768,768]{1,0:T(8,128)(2,1)} %bitcast.46, bf16[384,768]{1,0:T(8,128)(2,1)S(1)} %bitcast.48), kind=kOutput, calls=%fused_computation.58 | convolution fusion | flops 453869184 | bytes 3540480 | tf_op jit(solution)/shard_map/dot_general | solution.py:56
  80.2 0.3 multiply_reduce_fusion.3
  80.5 0.0 slice-start
  80.5 0.3 fusion.13.refs_6_
  80.8 0.0 slice-start.1
  80.8 2.8 %multiply_convert_fusion = (bf16[384,3072]{1,0:T(8,128)(2,1)S(1)}, f32[384,3072]{1,0:T(8,128)S(1)}) fusion(bf16[384,768]{1,0:T(8,128)(2,1)S(1)} %fusion.13.refs_6_, bf16[768,3072]{1,0:T(8,128)(2,1)S(1)} %bitcast.54), kind=kOutput, calls=%fused_computation.8 | convolution fusion | flops 1817837568 | bytes 12386304 | tf_op jit(solution)/shard_map/dot_general | solution.py:56
  83.7 2.1 %fusion.19 = (f32[384]{0:T(512)S(1)}, f32[384,768]{1,0:T(8,128)S(1)}) fusion(bf16[384,3072]{1,0:T(8,128)(2,1)S(1)} %get-tuple-element.68, bf16[3072,768]{1,0:T(8,128)(2,1)S(1)} %bitcast.58, f32[768]{0:T(1024)S(1)} %get-tuple-element.59, f32[768]{0:T(1024)S(1)} %get-tuple-element.73, f32[384]{0:T(512)S(1)} %add_rsqrt_fusion.1, ...), kind=kOutput, calls=%fused_computation.59 | convolution fusion | flops 1813708416 | bytes 9447936 | tf_op jit(solution)/shard_map/dot_general | solution.py:56
  85.8 0.3 multiply_reduce_fusion.2
  86.1 0.8 copy-done.1
  86.9 0.6 fusion.12
  87.5 1.3 fusion.9
  88.8 3.2 %fusion.5.refs_7_ = bf16[384,3072]{1,0:T(8,128)(2,1)S(1)} fusion(f32[384,3072]{1,0:T(8,128)S(1)} %get-tuple-element.69, bf16[3072,768]{1,0:T(8,128)(2,1)S(1)} %bitcast.59, f32[384,768]{1,0:T(8,128)S(1)} %get-tuple-element.62), kind=kOutput, calls=%fused_computation.7 | convolution fusion | flops 1824030720 | bytes 12976128 | tf_op jit(solution)/shard_map/dot_general | solution.py:66
  92.0 0.0 copy-start.2
  92.0 2.4 %multiply_reduce_fusion = (f32[768]{0:T(1024)S(1)}, f32[384]{0:T(512)S(1)}, f32[384]{0:T(512)S(1)}, f32[768]{0:T(1024)S(1)}, f32[384,768]{1,0:T(8,128)S(1)}) fusion(f32[384,768]{1,0:T(8,128)S(1)} %get-tuple-element.67, f32[384]{0:T(512)S(1)} %add_rsqrt_fusion.1, f32[384]{0:T(512)S(1)} %broadcast_multiply_fusion.5, f32[768]{0:T(1024)S(1)} %get-tuple-element.73, ...), kind=kOutput, calls=%fused_computation.24 | convolution fusion | flops 1814886144 | bytes 10632192 | tf_op jit(solution)/shard_map/dot_general | solution.py:66
  94.5 1.7 fusion.16
  96.1 0.6 pad_maximum_fusion.refs_1_
  96.8 4.3 %convolution_convert_fusion = bf16[3072,768]{1,0:T(8,128)(2,1)} fusion(bf16[384,3072]{1,0:T(8,128)(2,1)S(1)} %get-tuple-element.68, f32[384,768]{1,0:T(8,128)S(1)} %get-tuple-element.62), kind=kOutput, calls=%fused_computation.1 | convolution fusion | flops 1814593536 | bytes 8257536 | tf_op jit(solution)/shard_map/dot_general | solution.py:60
  101.1 103.5 %backward_half.1 = (f32[24,768]{1,0:T(8,128)}, f32[24,3072]{1,0:T(8,128)}, f32[96,768]{1,0:T(8,128)}, f32[4,768]{1,0:T(4,128)}, f32[2,192,768]{2,1,0:T(8,128)}, /*index=5*/f32[4,24,768]{2,1,0:T(8,128)}) custom-call(bf16[384,768]{1,0:T(8,128)(2,1)} %get-tuple-element.60.refs_0_, f32[4,768]{1,0:T(4,128)} %pad_maximum_fusion.refs_1_, ...), custom_call_target="tpu_custom_call" | custom-call | tf_op jit(solution)/shard_map/backward_half/pallas_call | solution.py:1367
  204.6 0.7 constant_dynamic-slice_fusion
  205.3 0.6 fusion.17
  205.9 1.2 reshape.127
  207.1 0.1 slice_bitcast_fusion
  207.2 0.2 copy.26
  207.4 0.9 reshape.128
  208.3 1.0 copy.35
  209.3 0.0 copy-done.9
  209.3 0.6 copy.36
  209.9 0.7 copy.37
  210.6 0.7 copy.38
  (31 shorter events, 0.1 us)
Async XLA Ops:
  0.6 0.8 copy-start
  0.6 5.9 %copy-start.6 = (bf16[192,2304]{1,0:T(8,128)(2,1)S(1)}, bf16[192,2304]{1,0:T(8,128)(2,1)}, u32[]{:S(2)}) copy-start(bf16[192,2304]{1,0:T(8,128)(2,1)} %param.13) | copy-start | bytes 2654212
  9.5 68.4 %copy-start.3 = (bf16[2,192,768]{2,1,0:T(8,128)(2,1)S(1)}, bf16[2,192,768]{2,1,0:T(8,128)(2,1)}, u32[]{:S(2)}) copy-start(bf16[2,192,768]{2,1,0:T(8,128)(2,1)} %refs_0_.1) | copy-start | bytes 1769476
  77.9 2.9 %copy-start.10 = (bf16[4,192,3072]{2,1,0:T(8,128)(2,1)S(1)}, bf16[4,192,3072]{2,1,0:T(8,128)(2,1)}, u32[]{:S(2)}) copy-start(bf16[4,192,3072]{2,1,0:T(8,128)(2,1)} %get-tuple-element.30) | copy-start | bytes 14155780
  80.5 3.2 %slice-start = ((s8[4718592]{0:T(1024)(128)(4,1)}), s8[4194304]{0:T(1024)(128)(4,1)S(1)}, s32[]{:S(2)}) async-start(s8[4718592]{0:T(1024)(128)(4,1)} %bitcast.56), calls=%async_computation | async-start | bytes 8388608
  80.8 2.9 %copy-start.4 = (bf16[384,768]{1,0:T(8,128)(2,1)}, bf16[384,768]{1,0:T(8,128)(2,1)S(1)}, u32[]{:S(2)}) copy-start(bf16[384,768]{1,0:T(8,128)(2,1)S(1)} %fusion.13.refs_6_) | copy-start | bytes 1769476
  80.8 2.9 %slice-start.1 = ((s8[4718592]{0:T(1024)(128)(4,1)}), s8[524288]{0:T(1024)(128)(4,1)S(1)}, s32[]{:S(2)}) async-start(s8[4718592]{0:T(1024)(128)(4,1)} %bitcast.56), calls=%async_computation.1 | async-start | bytes 1048576
  85.8 1.1 copy-start.1
  92.0 2.4 %copy-start.2 = (bf16[384,3072]{1,0:T(8,128)(2,1)}, bf16[384,3072]{1,0:T(8,128)(2,1)S(1)}, u32[]{:S(2)}) copy-start(bf16[384,3072]{1,0:T(8,128)(2,1)S(1)} %fusion.5.refs_7_) | copy-start | bytes 7077892
  205.9 2.4 %copy-start.5 = (f32[2,192,768]{2,1,0:T(8,128)S(1)}, f32[2,192,768]{2,1,0:T(8,128)}, u32[]{:S(2)}) copy-start(f32[2,192,768]{2,1,0:T(8,128)} %get-tuple-element.84) | copy-start | bytes 3538948
  208.3 1.0 copy-start.9
  208.3 1.7 copy-start.8
  208.3 2.4 %copy-start.7 = (f32[96,768]{1,0:T(8,128)S(1)}, f32[96,768]{1,0:T(8,128)}, u32[]{:S(2)}) copy-start(f32[96,768]{1,0:T(8,128)} %get-tuple-element.88) | copy-start | bytes 884740

commit v3 on v2

--- a/solution.py
+++ b/solution.py
@@ -578,11 +578,6 @@
     pl.semaphore_wait(pltpu.get_barrier_semaphore(), len(devices))
 
 
-def meet(devices):
-    greet(devices)
-    met(devices)
-
-
 def tile_tables(tile, rand_ref, segq_ref, blocks):
     wide = NH * TILE
     key = lax.broadcasted_iota(jnp.int32, (blocks, wide), 0)
@@ -614,6 +609,24 @@
     for i in range(steps):
         column = jnp.broadcast_to(segq[i].astype(F32), (8, TILE)).T[:, :1]
         segk[TILE * i : TILE * (i + 1), :] = jnp.broadcast_to(column, (TILE, TILE)).astype(jnp.int32)
+
+
+def fill_requests(requests, rand, half, group):
+    row = lax.broadcasted_iota(jnp.int32, (32, TILE), 0)
+    entry = lax.broadcasted_iota(jnp.int32, (32, TILE), 1)
+    slot = lax.rem(row, 8)
+    pick = jnp.logical_and(slot < 3, entry == 9 * group + 3 * (row // 8) + slot)
+    chosen = jnp.where(half == 0, requests[0], requests[1])
+    mine = nn(pick.astype(F32).astype(BF16), chosen)
+    steps = rand.shape[0]
+    block = lax.broadcasted_iota(jnp.int32, (TILE, steps * TILE), 0)
+    token = lax.broadcasted_iota(jnp.int32, (TILE, steps * TILE), 1)
+    spread = nn(mine.astype(BF16), (token // BLOCK == block).astype(F32).astype(BF16))
+    for i in range(steps):
+        for h in range(NH):
+            rand[i, :, TILE * h : TILE * (h + 1)] = spread[
+                8 * h : 8 * h + 3, TILE * i : TILE * (i + 1)
+            ].astype(jnp.int32)
 
 
 def forward_tile(tile, rand, segq, segk, qt, kn, vt, q3, tbuf, att, otile, lse):
@@ -658,8 +671,9 @@
 
 
 def forward_kernel(*refs):
-    (x, wg, wo, wu, wd, rand, segq), refs = refs[:7], refs[7:]
+    (x, w, wo, wu, wd, requests, seg), refs = refs[:7], refs[7:]
     outs, refs = refs[:14], refs[14:]
+    (rand, segq), refs = refs[:2], refs[2:]
     wof, wuf, wdf, att_out, otile_o, lse_o, segk_o, qn_o, kn_o, vn_o, qt_o, kt_o, xst_o, wgf_o = outs
     (xs, wgf, bo, bu, bd, att, home, otile, lse, segk), refs = refs[:10], refs[10:]
     (qn, kn, vn, qt, kt, vt, xst, q3, tbuf), refs = refs[:9], refs[9:]
@@ -678,7 +692,18 @@
     ]
     for load in loads:
         load.start()
-    meet([me.across_x, me.across_y] + [(d, lax.rem(t + k, 8)) for k in range(1, 8)])
+    friends = [me.across_x, me.across_y] + [(d, lax.rem(t + k, 8)) for k in range(1, 8)]
+    greet(friends)
+    shard = w.shape[0]
+    wrows = lambda index, start, size: pl.ds(pl.multiple_of(index * shard + start, size), size)
+    lane = lax.broadcasted_iota(jnp.int32, (shard, 256), 1)
+    for k in range(3):
+        first = w.shape[1] // 3 * k + 2 * NH * HEAD * lax.rem(z, 2) + TILE * c
+        window = w[:, pl.ds(pl.multiple_of(first, TILE), 256)].astype(F32)
+        moved = jnp.concatenate([window[:, HEAD:], window[:, :HEAD]], axis=1)
+        mine_k = jnp.where(lane < NH * HEAD, jnp.where(c == 0, window, moved), 0.0)
+        wgf[wrows(d, 0, shard), 256 * k : 256 * (k + 1)] = mine_k.astype(BF16)
+    met(friends)
     cps = Copies(send, recv)
     sent = []
 
@@ -690,15 +715,12 @@
     def rows_of(index):
         return pl.ds(pl.multiple_of(index * tok, tok), tok)
 
-    shard = wg.shape[0]
-    wrows = lambda index, start, size: pl.ds(pl.multiple_of(index * shard + start, size), size)
     half = shard // 2
-    top_half, low_half = pl.ds(0, half), pl.ds(half, half)
     my_top, my_low = wrows(d, 0, half), wrows(d, half, half)
-    wg_x0 = cps.to(wg.at[top_half], wgf.at[my_top], me.across_x)
-    wg_x1 = cps.to(wg.at[low_half], wgf.at[my_low], me.across_x)
-    wg_y0 = cps.to(wg.at[low_half], wgf.at[my_low], me.across_y)
-    wg_y1 = cps.to(wg.at[top_half], wgf.at[my_top], me.across_y)
+    wg_x0 = cps.to(wgf.at[my_top], wgf.at[my_top], me.across_x)
+    wg_x1 = cps.to(wgf.at[my_low], wgf.at[my_low], me.across_x)
+    wg_y0 = cps.to(wgf.at[my_low], wgf.at[my_low], me.across_y)
+    wg_y1 = cps.to(wgf.at[my_top], wgf.at[my_top], me.across_y)
     near = cps.to(x.at[mine], xs.at[rows_of(t)], me.at_z(me.pair_z))
     give = cps.to(x.at[mine], xs.at[rows_of(t)], me.partner)
     far = pltpu.make_async_remote_copy(
@@ -724,9 +746,12 @@
         begin(to_x, to_y)
 
     xs[rows_of(t), :] = x[mine]
-    wgf[wrows(d, 0, shard), :] = wg[...]
     q3[...] = jnp.zeros_like(q3)
+    seg_row = jnp.where(me.half == 0, seg[0:1, :], seg[1:2, :])
+    for i in range(steps):
+        segq[i] = seg_row[:, TILE * i : TILE * (i + 1)]
     fill_segments(segq, segk)
+    fill_requests(requests, rand, me.half, lax.rem(t, 4))
     keeps = []
     for i, (load, buf, full) in enumerate(zip(loads, (bo, bu, bd), (wof, wuf, wdf))):
         load.wait()
@@ -895,7 +920,7 @@
         copy.wait()
 
 
-def forward_half(x, wg, wo, wu, wd, rand, segq):
+def forward_half(x, w, wo, wu, wd, requests, seg):
     dp = lax.axis_size("dp")
     seq = lax.axis_size("seq")
     tok, features = x.shape[1:]
@@ -908,13 +933,15 @@
     return pl.pallas_call(
         forward_kernel,
         in_specs=[VMEMSPACE] * 2 + [ANYSPACE] * 3 + [VMEMSPACE] * 2,
-        out_specs=[ANYSPACE] * 3 + [VMEMSPACE] + [ANYSPACE] * 10,
+        out_specs=[ANYSPACE] * 3 + [VMEMSPACE] + [ANYSPACE] * 10 + [VMEMSPACE] * 2,
         out_shape=[
             stacked(wo), stacked(wu), stacked(wd), low(2 * tok, features),
             full(steps, NH * HEAD, TILE), full(steps, 1, NH * TILE),
             jax.ShapeDtypeStruct((length, TILE), jnp.int32),
             low(*nat), low(*nat), low(*nat), low(*tra), low(*tra),
             low(features, length), low(features, 768),
+            jax.ShapeDtypeStruct((steps, 3, NH * TILE), jnp.int32),
+            jax.ShapeDtypeStruct((steps, 1, TILE), jnp.int32),
         ],
         scratch_shapes=[
             pltpu.VMEM((length, features), BF16),
@@ -946,7 +973,7 @@
             collective_id=0, has_side_effects=True, vmem_limit_bytes=62 * 1024 * 1024
         ),
         name="forward_half",
-    )(x, wg, wo, wu, wd, rand, segq)
+    )(x, w, wo, wu, wd, requests, seg)
 
 
 def each(count, body):
@@ -1016,8 +1043,6 @@
     me = Place()
     c, z, x, y, t = me.c, me.z, me.x, me.y, me.t
     mine, other = me.half, 1 - me.half
-    is_middle = z == 1 + me.half
-    is_outer = z != 1 + me.half
     z_step = [lax.rem(z + k, 4) for k in (1, 2, 3)]
     tok = src.shape[1]
     loads = [
@@ -1197,7 +1222,7 @@
     events = {
         1: [step_one],
         2: [step_two],
-        5: [functools.partial(stage_a, up_work)],
+        4: [functools.partial(stage_a, up_work), functools.partial(cross, up_work)],
         7: [functools.partial(stage_b, out_work)],
         10: [functools.partial(stat_step, 3)],
     }
@@ -1225,7 +1250,8 @@
 
     dqkv[:, 256 : 256 + NH * HEAD] = (dk[...] * HEAD ** (-0.5)).astype(BF16)
     dqkv[:, 512 : 512 + NH * HEAD] = dv[...].astype(BF16)
-    order = [2 * other, 2 * other + 1, me.pair_z, z]
+    facing = 3 - z
+    order = [3 - me.pair_z, facing, me.pair_z, z]
     cores = []
 
     def partial_grad(k):
@@ -1243,32 +1269,15 @@
         cores[k].wait_recv()
         own_p[zz] = plus(part[zz, c], rp[zz]).astype(BF16)
 
-    up = [cps.to(own_p.at[2 * other + j], rb_p.at[j], me.at_z(me.pair_z)) for j in range(2)]
+    up = cps.to(own_p.at[3 - me.pair_z], rb_p, me.at_z(me.pair_z))
     near = cps.to(own_p.at[me.pair_z], ra_p, me.at_z(me.pair_z))
-    down_send, down_recv = cps.used, cps.used
-    cps.used += 2
-    down = [
-        pltpu.make_async_remote_copy(
-            src_ref=own_p.at[2 * other + j], dst_ref=ro, send_sem=send.at[down_send + j],
-            recv_sem=recv.at[down_recv], device_id=me.at_z(2 * other + j), device_id_type=MESH,
-        )
-        for j in range(2)
-    ]
+    over = cps.to(own_p.at[facing], ro, me.at_z(facing))
 
     partial_grad(0)
     partial_grad(1)
     merge_cores(0)
-    pl.when(is_outer)(up[0].start)
-    partial_grad(2)
-    merge_cores(1)
-    pl.when(is_outer)(up[1].start)
-    partial_grad(3)
+    begin(up)
     stage_b(down_work)
-    cross(up_work)
-    merge_cores(2)
-    begin(near)
-    merge_cores(3)
-    stage_c(out_work)
     loads[8].wait()
     half_rows = xst.shape[0] // 2
     for yy in range(2):
@@ -1277,16 +1286,18 @@
     bx = cps.to(dwg.at[:, 1 - x, 0:4], wb1, me.across_x)
     by = cps.to(dwg.at[1 - y, :, 4:8], wb2, me.across_y)
     begin(bx, by)
-
-    @pl.when(is_middle)
-    def _():
-        for j in range(2):
-            up[j].wait_recv()
-            own_p[2 * other + j] = plus(own_p[2 * other + j], rb_p[j]).astype(BF16)
-            down[j].start()
-
+    stage_b(up_work)
+    partial_grad(2)
+    merge_cores(1)
+    stage_c(out_work)
+    partial_grad(3)
+    merge_cores(2)
+    begin(near)
+    merge_cores(3)
     stage_c(down_work)
-    stage_b(up_work)
+    up.wait_recv()
+    own_p[facing] = plus(own_p[facing], rb_p[...]).astype(BF16)
+    begin(over)
     bx.wait_recv()
 
     def fold_x(i):
@@ -1324,28 +1335,21 @@
     near.wait_recv()
     more_loads[4].wait()
     ig[mine] = resid[mine] + plus(own_p[z], ra_p[...])
-    down[0].wait_recv()
+    over.wait_recv()
     ig[other] = resid[other] + ro[...].astype(F32)
     stage_d(out_work)
     stage_d(down_work)
     wr[t] = wc[t]
     for move in moves:
         move.wait_recv()
-    for g in range(4):
-        wq[g] = plus(wr[g], wr[4 + g])
+    sums = [plus(wr[g], wr[4 + g]) for g in range(4)]
+    width = NH * HEAD
+    for k in range(3):
+        part_k = [total[:, 256 * k : 256 * k + width] for total in sums]
+        wq[:, 4 * width * k : 4 * width * (k + 1)] = jnp.concatenate(part_k, axis=1)
     stage_d(up_work)
     for cp in sent + stat_all + [move for u, move in dat_moves] + [moves[0] for refs, moves in works]:
         cp.wait_send()
-
-    @pl.when(is_outer)
-    def _():
-        for cp in up:
-            cp.wait_send()
-
-    @pl.when(is_middle)
-    def _():
-        for cp in down:
-            cp.wait_send()
 
 
 def backward_half(da, stats, down_grad, rand, segq, extra, saved):
@@ -1372,7 +1376,7 @@
         + [
             jax.ShapeDtypeStruct(stats.shape, F32),
             jax.ShapeDtypeStruct((2, tok, features), F32),
-            jax.ShapeDtypeStruct((4, wrows, 768), F32),
+            jax.ShapeDtypeStruct((wrows, 3 * features), F32),
         ],
         scratch_shapes=bufs
         + [pltpu.VMEM(a.shape, a.dtype) for a in saved + extra]
@@ -1391,7 +1395,7 @@
             pltpu.VMEM((4, tok, features), BF16),
             pltpu.VMEM((4, tok, features), BF16),
             pltpu.VMEM((tok, features), BF16),
-            pltpu.VMEM((2, tok, features), BF16),
+            pltpu.VMEM((tok, features), BF16),
             pltpu.VMEM((tok, features), BF16),
             pltpu.VMEM((2, 2, 8, wrows, 768), BF16),
             pltpu.VMEM((2, 4, wrows, 768), BF16),
@@ -1417,22 +1421,12 @@
     seqs, tok, features = inputs.shape
     seq = lax.axis_size("seq")
     t = lax.axis_index("seq")
-    groups = seq // seqs
-    my_seq, my_group = t // groups, lax.rem(t, groups)
-    width = features // groups
-    shard = w_qkv.reshape(w_qkv.shape[0], 3, groups, width)
-    shard = lax.dynamic_index_in_dim(shard, my_group, 2, keepdims=False)
-    shard = jnp.pad(shard, ((0, 0), (0, 0), (0, 256 - width))).reshape(w_qkv.shape[0], 768)
-    steps = seq * tok // TILE
-    rand = lax.dynamic_slice_in_dim(
-        lax.dynamic_index_in_dim(rand_blocks, my_seq, 0, keepdims=False), my_group * NH, NH, 1
-    )
-    rand = rand.reshape(steps, TILE // BLOCK, NH, 3).transpose(0, 3, 2, 1)
-    rand = jnp.broadcast_to(rand[..., None], rand.shape + (BLOCK,)).reshape(steps, 3, NH * TILE)
-    seg = lax.dynamic_index_in_dim(segments, my_seq, 0, keepdims=False)
-    segq = seg.reshape(steps, 1, TILE)
-    wof, wuf, wdf, att_flat, otile, lse, segk, qn, kn, vn, qt, kt, xst, wgf = forward_half(
-        inputs, shard, w_out, w_up, w_down, rand, segq
+    requests = rand_blocks.transpose(0, 2, 3, 1).reshape(seqs, H * R, -1).astype(BF16)
+    requests = jnp.pad(
+        requests, ((0, 0), (0, TILE - requests.shape[1]), (0, TILE - requests.shape[2]))
+    )
+    wof, wuf, wdf, att_flat, otile, lse, segk, qn, kn, vn, qt, kt, xst, wgf, rand, segq = forward_half(
+        inputs, w_qkv, w_out, w_up, w_down, requests, segments
     )
     full_out = wof.reshape(features, features)
     full_up = wuf.reshape(features, -1)
@@ -1464,13 +1458,12 @@
         (wof, hidden_low, grad_pre, att_flat, grad_resid_one.reshape(seqs, tok, features)),
         (kn, vn, kt, segk, qn, qt, otile, lse, xst, wgf),
     )
-    wq = wq.reshape(groups, features // 32, 3, 256)[..., :width].transpose(1, 2, 0, 3)
     mine = lax.axis_index("dp") * seq + t
     stats = lax.dynamic_slice_in_dim(stats, mine * (features // 32), features // 32, 1)
     return (
         result.astype(BF16).reshape(seqs, tok, features),
         ig,
-        wq.reshape(features // 32, 3 * features),
+        wq,
         out_sum,
         up_sum,
         down_sum,

time: 212 us -> 205 us (0.967)
  local copies, waits for them, and re-layouts: 14.9 us -> 8.89 us
    reshape x5 -> x0, local copies, waits for them, and re-layouts: 5.26 us -> none  [the longest x1 1.31 us: head_layout(): segq = seg.reshape(steps, 1, TILE)]
    unnamed x32 -> x27, local copies, waits for them, and re-layouts: 5.63 us -> 6 us
where the time goes in v3:
time: 205 us
  Pallas kernels  171 us (83%)
  matrix products  17.4 us (8%)
  local copies, waits for them, and re-layouts  8.89 us (4%)
  other arithmetic  7.16 us (3%)
    pallas_call x1, Pallas kernels, backward_half(): pl.pallas_call(backward_kernel, in_specs=[VMEMSPACE] * 2 + [ANYSPACE] + [...  102 us
    pallas_call x1, Pallas kernels, forward_half(): pl.pallas_call(forward_kernel, in_specs=[VMEMSPACE] * 2 + [ANYSPACE] * 3...  68.6 us
    dot_general x3, matrix products, product(): return jnp.dot(left_side, right_side, preferred_element_type=jnp.float32)  7.3 us
    unnamed x27, local copies, waits for them, and re-layouts  6 us
    dot_general x2, matrix products, product_nt(): lax.dot_general(left_side, right_side, (((1,), (1,)), ((), ())), preferre...  5.77 us
    dot_general x1, matrix products, product_tn(): lax.dot_general(left_side, right_side, (((0,), (0,)), ((), ())), preferre...  4.29 us

profile of v3, /device:TPU:0, one launch (start us, length us, event | category | flops | bytes accessed | tf_op | source)
XLA Modules:
  0.0 204.8 jit_solution(11541191565127674110)
XLA Ops:
  0.6 0.8 slice_reduce_fusion
  1.5 1.4 convert_reduce_fusion
  2.9 0.1 div.31
  3.0 0.8 convert_element_type.50
  3.8 0.6 pad.4.refs_5_
  4.4 0.0 copy-start.1
  4.4 68.6 %forward_half.1 = (bf16[4,192,768]{2,1,0:T(8,128)(2,1)}, bf16[4,192,3072]{2,1,0:T(8,128)(2,1)}, bf16[4,768,768]{2,1,0:T(8,128)(2,1)}, bf16[384,768]{1,0:T(8,128)...) custom-call(bf16[2,192,768]{2,1,0:T(8,128)(2,1)} %refs_0_.1, ...), custom_call_target="tpu_custom_call" | custom-call | tf_op jit(solution)/shard_map/forward_half/pallas_call | solution.py:933
  73.0 0.0 copy-done.1
  73.0 0.0 copy-start.8
  73.0 2.3 %fusion.18 = (f32[384]{0:T(512)S(1)}, f32[384,768]{1,0:T(8,128)S(1)}) fusion(bf16[384,768]{1,0:T(8,128)(2,1)} %get-tuple-element.30.refs_8_, bf16[768,768]{1,0:T(8,128)(2,1)} %bitcast.37, bf16[384,768]{1,0:T(8,128)(2,1)S(1)} %bitcast.39), kind=kOutput, calls=%fused_computation.53 | convolution fusion | flops 453869184 | bytes 3540480 | tf_op jit(solution)/shard_map/dot_general | solution.py:56
  75.4 0.3 multiply_reduce_fusion.3
  75.6 0.0 slice-start
  75.6 0.3 fusion.13.refs_6_
  75.9 0.0 copy-done.8
  75.9 0.0 copy-start.3
  75.9 0.0 slice-start.1
  75.9 2.9 %multiply_convert_fusion = (bf16[384,3072]{1,0:T(8,128)(2,1)S(1)}, f32[384,3072]{1,0:T(8,128)S(1)}) fusion(bf16[384,768]{1,0:T(8,128)(2,1)S(1)} %fusion.13.refs_6_, bf16[768,3072]{1,0:T(8,128)(2,1)S(1)} %bitcast.42), kind=kOutput, calls=%fused_computation.8 | convolution fusion | flops 1817837568 | bytes 12386304 | tf_op jit(solution)/shard_map/dot_general | solution.py:56
  78.8 0.0 copy-done.3
  78.8 0.0 slice-done
  78.8 0.0 slice-done.1
  78.8 2.1 %fusion.19 = (f32[384]{0:T(512)S(1)}, f32[384,768]{1,0:T(8,128)S(1)}) fusion(bf16[384,3072]{1,0:T(8,128)(2,1)S(1)} %get-tuple-element.72, bf16[3072,768]{1,0:T(8,128)(2,1)S(1)} %bitcast.46, f32[768]{0:T(1024)S(1)} %get-tuple-element.63, f32[768]{0:T(1024)S(1)} %get-tuple-element.77, f32[384]{0:T(512)S(1)} %add_rsqrt_fusion.1, ...), kind=kOutput, calls=%fused_computation.54 | convolution fusion | flops 1813708416 | bytes 9447936 | tf_op jit(solution)/shard_map/dot_general | solution.py:56
  81.0 0.0 copy-start
  81.0 0.3 multiply_reduce_fusion.2
  81.3 0.8 copy-done
  82.0 0.6 fusion.12
  82.6 1.3 fusion.9
  83.9 3.3 %fusion.5.refs_7_ = bf16[384,3072]{1,0:T(8,128)(2,1)S(1)} fusion(f32[384,3072]{1,0:T(8,128)S(1)} %get-tuple-element.73, bf16[3072,768]{1,0:T(8,128)(2,1)S(1)} %bitcast.47, f32[384,768]{1,0:T(8,128)S(1)} %get-tuple-element.66), kind=kOutput, calls=%fused_computation.7 | convolution fusion | flops 1824030720 | bytes 12976128 | tf_op jit(solution)/shard_map/dot_general | solution.py:66
  87.3 0.0 copy-start.2
  87.3 2.4 %multiply_reduce_fusion = (f32[768]{0:T(1024)S(1)}, f32[384]{0:T(512)S(1)}, f32[384]{0:T(512)S(1)}, f32[768]{0:T(1024)S(1)}, f32[384,768]{1,0:T(8,128)S(1)}) fusion(f32[384,768]{1,0:T(8,128)S(1)} %get-tuple-element.71, f32[384]{0:T(512)S(1)} %add_rsqrt_fusion.1, f32[384]{0:T(512)S(1)} %broadcast_multiply_fusion.5, f32[768]{0:T(1024)S(1)} %get-tuple-element.77, ...), kind=kOutput, calls=%fused_computation.24 | convolution fusion | flops 1814886144 | bytes 10632192 | tf_op jit(solution)/shard_map/dot_general | solution.py:66
  89.7 0.0 copy-done.2
  89.7 1.7 fusion.16
  91.4 0.6 pad_maximum_fusion.refs_1_
  92.0 4.3 %convolution_convert_fusion = bf16[3072,768]{1,0:T(8,128)(2,1)} fusion(bf16[384,3072]{1,0:T(8,128)(2,1)S(1)} %get-tuple-element.72, f32[384,768]{1,0:T(8,128)S(1)} %get-tuple-element.66), kind=kOutput, calls=%fused_computation.1 | convolution fusion | flops 1814593536 | bytes 8257536 | tf_op jit(solution)/shard_map/dot_general | solution.py:60
  96.3 101.9 %backward_half.1 = (f32[24,768]{1,0:T(8,128)}, f32[24,3072]{1,0:T(8,128)}, f32[96,768]{1,0:T(8,128)}, f32[4,768]{1,0:T(4,128)}, f32[2,192,768]{2,1,0:T(8,128)}, /*index=5*/f32[24,2304]{1,0:T(8,128)}) custom-call(bf16[384,768]{1,0:T(8,128)(2,1)} %get-tuple-element.64.refs_0_, f32[4,768]{1,0:T(4,128)} %pad_maximum_fusion.refs_1_, ...), custom_call_target="tpu_custom_call" | custom-call | tf_op jit(solution)/shard_map/backward_half/pallas_call | solution.py:1371
  198.2 0.8 constant_dynamic-slice_fusion
  199.0 0.6 fusion.17
  199.6 0.0 copy-start.6
  199.6 0.0 copy-start.7
  199.6 0.0 copy-start.5
  199.6 2.4 %copy.25 = f32[2,192,768]{2,1,0:T(8,128)} copy(f32[2,192,768]{2,1,0:T(8,128)} %get-tuple-element.88) | data formatting | bytes 2359296
  202.0 0.0 copy-done.6
  202.0 0.7 copy.26
  202.7 0.0 copy-done.7
  202.7 0.6 copy.27
  203.4 0.0 copy-done.5
  203.4 0.7 copy.28
  204.1 0.0 copy-done.4
  204.1 0.7 copy.29
  (15 shorter events, 0.1 us)
Async XLA Ops:
  4.4 68.6 %copy-start.1 = (bf16[2,192,768]{2,1,0:T(8,128)(2,1)S(1)}, bf16[2,192,768]{2,1,0:T(8,128)(2,1)}, u32[]{:S(2)}) copy-start(bf16[2,192,768]{2,1,0:T(8,128)(2,1)} %refs_0_.1) | copy-start | bytes 1769476
  73.0 2.9 %copy-start.8 = (bf16[4,192,3072]{2,1,0:T(8,128)(2,1)S(1)}, bf16[4,192,3072]{2,1,0:T(8,128)(2,1)}, u32[]{:S(2)}) copy-start(bf16[4,192,3072]{2,1,0:T(8,128)(2,1)} %get-tuple-element.32) | copy-start | bytes 14155780
  75.6 3.2 %slice-start = ((s8[4718592]{0:T(1024)(128)(4,1)}), s8[4194304]{0:T(1024)(128)(4,1)S(1)}, s32[]{:S(2)}) async-start(s8[4718592]{0:T(1024)(128)(4,1)} %bitcast.44), calls=%async_computation | async-start | bytes 8388608
  75.9 2.9 %copy-start.3 = (bf16[384,768]{1,0:T(8,128)(2,1)}, bf16[384,768]{1,0:T(8,128)(2,1)S(1)}, u32[]{:S(2)}) copy-start(bf16[384,768]{1,0:T(8,128)(2,1)S(1)} %fusion.13.refs_6_) | copy-start | bytes 1769476
  75.9 2.9 %slice-start.1 = ((s8[4718592]{0:T(1024)(128)(4,1)}), s8[524288]{0:T(1024)(128)(4,1)S(1)}, s32[]{:S(2)}) async-start(s8[4718592]{0:T(1024)(128)(4,1)} %bitcast.44), calls=%async_computation.1 | async-start | bytes 1048576
  81.0 1.1 copy-start
  87.3 2.4 %copy-start.2 = (bf16[384,3072]{1,0:T(8,128)(2,1)}, bf16[384,3072]{1,0:T(8,128)(2,1)S(1)}, u32[]{:S(2)}) copy-start(bf16[384,3072]{1,0:T(8,128)(2,1)S(1)} %fusion.5.refs_7_) | copy-start | bytes 7077892
  199.6 2.5 %copy-start.6 = (f32[24,2304]{1,0:T(8,128)S(1)}, f32[24,2304]{1,0:T(8,128)}, u32[]{:S(2)}) copy-start(f32[24,2304]{1,0:T(8,128)} %get-tuple-element.89) | copy-start | bytes 663556
  199.6 3.1 %copy-start.7 = (f32[24,768]{1,0:T(8,128)S(1)}, f32[24,768]{1,0:T(8,128)}, u32[]{:S(2)}) copy-start(f32[24,768]{1,0:T(8,128)} %get-tuple-element.90) | copy-start | bytes 221188
  199.6 3.8 %copy-start.5 = (f32[24,3072]{1,0:T(8,128)S(1)}, f32[24,3072]{1,0:T(8,128)}, u32[]{:S(2)}) copy-start(f32[24,3072]{1,0:T(8,128)} %get-tuple-element.91) | copy-start | bytes 884740
  199.6 4.5 %copy-start.4 = (f32[96,768]{1,0:T(8,128)S(1)}, f32[96,768]{1,0:T(8,128)}, u32[]{:S(2)}) copy-start(f32[96,768]{1,0:T(8,128)} %get-tuple-element.92) | copy-start | bytes 884740

commit v4 on v3

--- a/solution.py
+++ b/solution.py
@@ -511,7 +511,7 @@
 
 TILE = 128
 NH = 3
-CH = 256
+CH = 512
 LOG2E = 1.4426950408889634
 SCALE2 = HEAD ** (-0.5) * LOG2E
 NEG = -1e30

time: 205 us -> 203 us (level)
  no operation moved by 1% of the time
where the time goes in v4:
time: 203 us
  Pallas kernels  169 us (83%)
  matrix products  17.3 us (9%)
  local copies, waits for them, and re-layouts  8.89 us (4%)
  other arithmetic  7.16 us (4%)
    pallas_call x1, Pallas kernels, backward_half(): pl.pallas_call(backward_kernel, in_specs=[VMEMSPACE] * 2 + [ANYSPACE] + [...  101 us
    pallas_call x1, Pallas kernels, forward_half(): pl.pallas_call(forward_kernel, in_specs=[VMEMSPACE] * 2 + [ANYSPACE] * 3...  67.9 us
    dot_general x3, matrix products, product(): return jnp.dot(left_side, right_side, preferred_element_type=jnp.float32)  7.29 us
    unnamed x27, local copies, waits for them, and re-layouts  6 us
    dot_general x2, matrix products, product_nt(): lax.dot_general(left_side, right_side, (((1,), (1,)), ((), ())), preferre...  5.77 us
    dot_general x1, matrix products, product_tn(): lax.dot_general(left_side, right_side, (((0,), (0,)), ((), ())), preferre...  4.29 us

profile of v4, /device:TPU:0, one launch (start us, length us, event | category | flops | bytes accessed | tf_op | source)
XLA Modules:
  0.0 203.1 jit_solution(2938952736762147723)
XLA Ops:
  0.6 0.8 slice_reduce_fusion
  1.5 1.4 convert_reduce_fusion
  2.9 0.1 div.31
  3.0 0.8 convert_element_type.50
  3.8 0.6 pad.4.refs_5_
  4.4 0.0 copy-start.1
  4.4 67.9 %forward_half.1 = (bf16[4,192,768]{2,1,0:T(8,128)(2,1)}, bf16[4,192,3072]{2,1,0:T(8,128)(2,1)}, bf16[4,768,768]{2,1,0:T(8,128)(2,1)}, bf16[384,768]{1,0:T(8,128)...) custom-call(bf16[2,192,768]{2,1,0:T(8,128)(2,1)} %refs_0_.1, ...), custom_call_target="tpu_custom_call" | custom-call | tf_op jit(solution)/shard_map/forward_half/pallas_call | solution.py:933
  72.3 0.0 copy-done.1
  72.3 0.0 copy-start.8
  72.3 2.3 %fusion.18 = (f32[384]{0:T(512)S(1)}, f32[384,768]{1,0:T(8,128)S(1)}) fusion(bf16[384,768]{1,0:T(8,128)(2,1)} %get-tuple-element.30.refs_8_, bf16[768,768]{1,0:T(8,128)(2,1)} %bitcast.37, bf16[384,768]{1,0:T(8,128)(2,1)S(1)} %bitcast.39), kind=kOutput, calls=%fused_computation.53 | convolution fusion | flops 453869184 | bytes 3540480 | tf_op jit(solution)/shard_map/dot_general | solution.py:56
  74.6 0.3 multiply_reduce_fusion.3
  74.9 0.0 slice-start
  74.9 0.3 fusion.13.refs_6_
  75.2 0.0 copy-done.8
  75.2 0.0 copy-start.3
  75.2 0.0 slice-start.1
  75.2 2.9 %multiply_convert_fusion = (bf16[384,3072]{1,0:T(8,128)(2,1)S(1)}, f32[384,3072]{1,0:T(8,128)S(1)}) fusion(bf16[384,768]{1,0:T(8,128)(2,1)S(1)} %fusion.13.refs_6_, bf16[768,3072]{1,0:T(8,128)(2,1)S(1)} %bitcast.42), kind=kOutput, calls=%fused_computation.8 | convolution fusion | flops 1817837568 | bytes 12386304 | tf_op jit(solution)/shard_map/dot_general | solution.py:56
  78.1 0.0 copy-done.3
  78.1 0.0 slice-done
  78.1 0.0 slice-done.1
  78.1 2.1 %fusion.19 = (f32[384]{0:T(512)S(1)}, f32[384,768]{1,0:T(8,128)S(1)}) fusion(bf16[384,3072]{1,0:T(8,128)(2,1)S(1)} %get-tuple-element.72, bf16[3072,768]{1,0:T(8,128)(2,1)S(1)} %bitcast.46, f32[768]{0:T(1024)S(1)} %get-tuple-element.63, f32[768]{0:T(1024)S(1)} %get-tuple-element.77, f32[384]{0:T(512)S(1)} %add_rsqrt_fusion.1, ...), kind=kOutput, calls=%fused_computation.54 | convolution fusion | flops 1813708416 | bytes 9447936 | tf_op jit(solution)/shard_map/dot_general | solution.py:56
  80.2 0.3 multiply_reduce_fusion.2
  80.5 0.8 copy-done
  81.3 0.6 fusion.12
  81.9 1.3 fusion.9
  83.2 3.3 %fusion.5.refs_7_ = bf16[384,3072]{1,0:T(8,128)(2,1)S(1)} fusion(f32[384,3072]{1,0:T(8,128)S(1)} %get-tuple-element.73, bf16[3072,768]{1,0:T(8,128)(2,1)S(1)} %bitcast.47, f32[384,768]{1,0:T(8,128)S(1)} %get-tuple-element.66), kind=kOutput, calls=%fused_computation.7 | convolution fusion | flops 1824030720 | bytes 12976128 | tf_op jit(solution)/shard_map/dot_general | solution.py:66
  86.5 0.0 copy-start.2
  86.5 2.4 %multiply_reduce_fusion = (f32[768]{0:T(1024)S(1)}, f32[384]{0:T(512)S(1)}, f32[384]{0:T(512)S(1)}, f32[768]{0:T(1024)S(1)}, f32[384,768]{1,0:T(8,128)S(1)}) fusion(f32[384,768]{1,0:T(8,128)S(1)} %get-tuple-element.71, f32[384]{0:T(512)S(1)} %add_rsqrt_fusion.1, f32[384]{0:T(512)S(1)} %broadcast_multiply_fusion.5, f32[768]{0:T(1024)S(1)} %get-tuple-element.77, ...), kind=kOutput, calls=%fused_computation.24 | convolution fusion | flops 1814886144 | bytes 10632192 | tf_op jit(solution)/shard_map/dot_general | solution.py:66
  89.0 0.0 copy-done.2
  89.0 1.7 fusion.16
  90.7 0.6 pad_maximum_fusion.refs_1_
  91.3 4.3 %convolution_convert_fusion = bf16[3072,768]{1,0:T(8,128)(2,1)} fusion(bf16[384,3072]{1,0:T(8,128)(2,1)S(1)} %get-tuple-element.72, f32[384,768]{1,0:T(8,128)S(1)} %get-tuple-element.66), kind=kOutput, calls=%fused_computation.1 | convolution fusion | flops 1814593536 | bytes 8257536 | tf_op jit(solution)/shard_map/dot_general | solution.py:60
  95.6 100.9 %backward_half.1 = (f32[24,768]{1,0:T(8,128)}, f32[24,3072]{1,0:T(8,128)}, f32[96,768]{1,0:T(8,128)}, f32[4,768]{1,0:T(4,128)}, f32[2,192,768]{2,1,0:T(8,128)}, /*index=5*/f32[24,2304]{1,0:T(8,128)}) custom-call(bf16[384,768]{1,0:T(8,128)(2,1)} %get-tuple-element.64.refs_0_, f32[4,768]{1,0:T(4,128)} %pad_maximum_fusion.refs_1_, ...), custom_call_target="tpu_custom_call" | custom-call | tf_op jit(solution)/shard_map/backward_half/pallas_call | solution.py:1371
  196.5 0.8 constant_dynamic-slice_fusion
  197.3 0.6 fusion.17
  197.8 0.0 copy-start.6
  197.9 0.0 copy-start.7
  197.9 0.0 copy-start.5
  197.9 0.0 copy-start.4
  197.9 2.4 %copy.25 = f32[2,192,768]{2,1,0:T(8,128)} copy(f32[2,192,768]{2,1,0:T(8,128)} %get-tuple-element.88) | data formatting | bytes 2359296
  200.3 0.0 copy-done.6
  200.3 0.7 copy.26
  201.0 0.0 copy-done.7
  201.0 0.6 copy.27
  201.6 0.0 copy-done.5
  201.6 0.7 copy.28
  202.3 0.0 copy-done.4
  202.3 0.7 copy.29
  (15 shorter events, 0.1 us)
Async XLA Ops:
  4.4 67.9 %copy-start.1 = (bf16[2,192,768]{2,1,0:T(8,128)(2,1)S(1)}, bf16[2,192,768]{2,1,0:T(8,128)(2,1)}, u32[]{:S(2)}) copy-start(bf16[2,192,768]{2,1,0:T(8,128)(2,1)} %refs_0_.1) | copy-start | bytes 1769476
  72.3 2.9 %copy-start.8 = (bf16[4,192,3072]{2,1,0:T(8,128)(2,1)S(1)}, bf16[4,192,3072]{2,1,0:T(8,128)(2,1)}, u32[]{:S(2)}) copy-start(bf16[4,192,3072]{2,1,0:T(8,128)(2,1)} %get-tuple-element.32) | copy-start | bytes 14155780
  74.9 3.2 %slice-start = ((s8[4718592]{0:T(1024)(128)(4,1)}), s8[4194304]{0:T(1024)(128)(4,1)S(1)}, s32[]{:S(2)}) async-start(s8[4718592]{0:T(1024)(128)(4,1)} %bitcast.44), calls=%async_computation | async-start | bytes 8388608
  75.2 2.9 %copy-start.3 = (bf16[384,768]{1,0:T(8,128)(2,1)}, bf16[384,768]{1,0:T(8,128)(2,1)S(1)}, u32[]{:S(2)}) copy-start(bf16[384,768]{1,0:T(8,128)(2,1)S(1)} %fusion.13.refs_6_) | copy-start | bytes 1769476
  75.2 2.9 %slice-start.1 = ((s8[4718592]{0:T(1024)(128)(4,1)}), s8[524288]{0:T(1024)(128)(4,1)S(1)}, s32[]{:S(2)}) async-start(s8[4718592]{0:T(1024)(128)(4,1)} %bitcast.44), calls=%async_computation.1 | async-start | bytes 1048576
  80.2 1.1 copy-start
  86.5 2.4 %copy-start.2 = (bf16[384,3072]{1,0:T(8,128)(2,1)}, bf16[384,3072]{1,0:T(8,128)(2,1)S(1)}, u32[]{:S(2)}) copy-start(bf16[384,3072]{1,0:T(8,128)(2,1)S(1)} %fusion.5.refs_7_) | copy-start | bytes 7077892
  197.8 2.5 %copy-start.6 = (f32[24,2304]{1,0:T(8,128)S(1)}, f32[24,2304]{1,0:T(8,128)}, u32[]{:S(2)}) copy-start(f32[24,2304]{1,0:T(8,128)} %get-tuple-element.89) | copy-start | bytes 663556
  197.9 3.1 %copy-start.7 = (f32[24,768]{1,0:T(8,128)S(1)}, f32[24,768]{1,0:T(8,128)}, u32[]{:S(2)}) copy-start(f32[24,768]{1,0:T(8,128)} %get-tuple-element.90) | copy-start | bytes 221188
  197.9 3.8 %copy-start.5 = (f32[24,3072]{1,0:T(8,128)S(1)}, f32[24,3072]{1,0:T(8,128)}, u32[]{:S(2)}) copy-start(f32[24,3072]{1,0:T(8,128)} %get-tuple-element.91) | copy-start | bytes 884740
  197.9 4.5 %copy-start.4 = (f32[96,768]{1,0:T(8,128)S(1)}, f32[96,768]{1,0:T(8,128)}, u32[]{:S(2)}) copy-start(f32[96,768]{1,0:T(8,128)} %get-tuple-element.92) | copy-start | bytes 884740
